TPU v7x, 512 devices: a whole 4x4x16 slice. The times are simulated.
512 devices in a mesh: grp: 32 (over x, y, z_hi), tile: 16 (over z_lo, core).
Axes of the slice: x: 4, y: 4, z: 16 (z_hi: 2, z_lo: 8; z = z_hi * 8 + z_lo), core: 2. Of those that a mesh axis runs over, the one named last changes fastest.
Arguments:
- log_cond: float32 [32, 128, 32, 128], P('grp', 'tile'), may hold values from -3 to 3
- potential: float32 [32, 128, 32, 128], P('grp', 'tile'), may hold values from -6 to 6
- noise: float32 [2, 32, 128, 32, 128], P(None, 'grp', 'tile'), may hold values from -3 to 3
- source: float32 [128, 32, 128], P('tile'), may hold values from -6 to 6
- parents: int32 [32], replicated, may hold values from 0 to 31
- accept: int32 [2, 32], P(None, 'grp'), may hold values 0 or 1
- weights: float32 [32], P('grp'), may hold values from 0.1 to 10
Outputs:
- conduct_out: float32 [32, 128, 32, 128], P('grp', 'tile')
- potential_out: float32 [32, 128, 32, 128], P('grp', 'tile')
- moments: float32 [1024, 1024], P('tile')
Inputs may be any that keep to these rules, and one draw needn't show every extreme that they name: `parents`: parent indices of offspring.
All inputs are finite; a program needn't handle non-finite values. No bound on the sum of `accept` on one device may be relied on, other than what follows from the above.
Results may differ from a plain program's by a relative error of at most 0.0001.
Values sent between devices are 32-bit elements; how exact they have to be, the bound alone decides.
A program may use at most 64 MiB of HBM per device.

v0:
```python
import jax
import jax.numpy as jnp
from jax import lax
from jax.sharding import PartitionSpec as P

prior_keep = 0.8
prior_fresh = 0.6
relax_weight = 0.8


def with_halo(block, sides, width):
    for axis, dim in sides:
        count = lax.axis_size(axis)
        forward = [(i, i + 1) for i in range(count - 1)]
        backward = [(target, source) for source, target in forward]
        low = lax.ppermute(
            lax.slice_in_dim(block, block.shape[dim] - width, None, axis=dim), axis, forward
        )
        high = lax.ppermute(lax.slice_in_dim(block, 0, width, axis=dim), axis, backward)
        block = jnp.concatenate([low, block, high], axis=dim)
    return block


def neighbours(padded):
    return [
        padded[2:, 1:-1, 1:-1],
        padded[:-2, 1:-1, 1:-1],
        padded[1:-1, 2:, 1:-1],
        padded[1:-1, :-2, 1:-1],
        padded[1:-1, 1:-1, 2:],
        padded[1:-1, 1:-1, :-2],
    ]


def relax_sweep(cond_ext, pot_ext, source):
    cond_pad = jnp.pad(cond_ext, ((0, 0), (1, 1), (1, 1)))
    pot_pad = jnp.pad(pot_ext, ((0, 0), (1, 1), (1, 1)))
    conductivity = jnp.exp(cond_pad)
    centre_k = conductivity[1:-1, 1:-1, 1:-1]
    centre = pot_pad[1:-1, 1:-1, 1:-1]
    flux_sum = jnp.zeros_like(centre)
    coef_sum = jnp.zeros_like(centre)
    for near_k, near_v in zip(neighbours(conductivity), neighbours(pot_pad)):
        face = 0.5 * (centre_k + near_k)
        flux_sum = flux_sum + face * near_v
        coef_sum = coef_sum + face
    return (1.0 - relax_weight) * centre + relax_weight * (source + flux_sum) / coef_sum


def local(log_cond, potential, noise, source, parents, accept, weights):
    mine = lax.axis_index("grp")
    bundle = jnp.stack([log_cond[0], potential[0]])
    parent = parents[mine]
    pieces = lax.all_gather(bundle[None], "grp", axis=0, tiled=True)
    owners = jnp.arange(pieces.shape[0], dtype=jnp.int32)
    chosen = jnp.where((owners == parent)[:, None, None, None, None], pieces, 0.0)
    moved = jnp.sum(chosen, axis=0)
    conduct = moved[0]
    pot = moved[1]
    width = conduct.shape[0]
    for move_index in range(noise.shape[0]):
        proposal = prior_keep * conduct + prior_fresh * noise[move_index, 0]
        extended = with_halo(jnp.stack([proposal, pot]), (("tile", 1),), 1)
        relaxed_once = relax_sweep(extended[0], extended[1], source)
        pot_ext = with_halo(relaxed_once, (("tile", 0),), 1)
        relaxed_twice = relax_sweep(extended[0], pot_ext, source)
        accepted = accept[move_index, 0] > 0
        conduct = jnp.where(accepted, proposal, conduct)
        pot = jnp.where(accepted, relaxed_twice, pot)
    weight_sum = lax.psum(jnp.sum(weights), "grp")
    share = weights[0] / weight_sum
    traces = jnp.transpose(pot, (1, 0, 2)).reshape(pot.shape[1], width * pot.shape[2])
    product = lax.dot_general(
        traces,
        traces,
        (((0,), (0,)), ((), ())),
        precision=lax.Precision.HIGHEST,
        preferred_element_type=jnp.float32,
    )
    partial_rows = lax.psum_scatter(share * product, "tile", scatter_dimension=0, tiled=True)
    moments = lax.psum(partial_rows, "grp")
    return (conduct[None], pot[None], moments)


def solution(mesh):
    placed = (
        P("grp", "tile", None, None),
        P("grp", "tile", None, None),
        P(None, "grp", "tile", None, None),
        P("tile", None, None),
        P(),
        P(None, "grp"),
        P("grp"),
    )
    return jax.shard_map(
        local,
        mesh=mesh,
        in_specs=placed,
        out_specs=(P("grp", "tile", None, None), P("grp", "tile", None, None), P("tile", None)),
        check_vma=False,
    )
```

profile of v0, /device:TPU:1, one launch (start us, length us, event | category | flops | bytes accessed | tf_op | source)
XLA Modules:
  0.0 1138.5 jit_solution(12140395760338257270)
XLA Ops:
  7.2 0.0 all-gather.3.cloned.1.call-start
  7.2 1.7 pad_maximum_fusion.2
  8.9 0.0 all-gather.3.cloned.1.call-update
  8.9 0.0 reduce-scatter.2.cloned.1.call-start
  9.0 1.3 fusion.101
  11.6 1.2 dynamic_slice.3
  12.8 0.6 iota_compare_fusion.4
  13.5 243.4 %all-gather.3.cloned.1.call-done = f32[64,8,32,128]{3,2,1,0:T(8,128)} async-done(((f32[2,8,32,128]{3,2,1,0:T(8,128)}), f32[64,8,32,128]{3,2,1,0:T(8,128)}) %all-gather.3.cloned.1.call-update) | async-done | bytes 8388624 | tf_op jit(solution)/shard_map/all_gather | solution.py:54
  256.9 0.0 copy-start.2
  256.9 0.0 copy-start
  256.9 4.6 select_reduce_fusion
  261.6 0.0 copy-done.2
  261.6 0.7 broadcast_select_fusion
  262.3 4.2 collective-permute-start
  266.5 5.8 collective-permute-start.1
  272.3 0.0 collective-permute-done
  272.3 0.8 collective-permute-done.1
  273.2 0.0 copy-done
  273.2 0.3 fusion.11
  273.5 2.3 collective-permute-start.2
  275.8 8.2 collective-permute-start.3
  284.0 0.0 collective-permute-done.2
  284.0 0.8 collective-permute-done.3
  284.8 0.2 select_maximum_fusion.2
  285.0 0.3 fusion.85
  285.3 4.5 collective-permute-start.4
  289.9 1.9 collective-permute-start.5
  291.8 0.0 collective-permute-done.4
  291.8 4.7 collective-permute-done.5
  296.6 0.3 fusion.23
  296.9 1.9 collective-permute-start.6
  298.8 3.6 collective-permute-start.7
  302.5 136.7 %psum.14 = f32[]{:T(128)} all-reduce(f32[]{:T(128)} %bitcast.17), channel_id=1, replica_groups=mesh['grp'=32,'tile'=16] {'grp'}, use_global_device_ids=true, to_apply=%region_1.2 | all-reduce | flops 1 | bytes 8 | tf_op jit(solution)/shard_map/psum | solution.py:70
  440.5 0.0 collective-permute-done.6
  440.5 0.0 collective-permute-done.7
  440.5 0.2 select_maximum_fusion
  440.7 0.3 fusion.66
  441.0 0.0 copy-start.1
  441.0 5.1 convolution_multiply_fusion
  446.1 0.0 reduce-scatter.2.cloned.1.call-update
  446.1 0.0 copy-done.1
  446.1 0.0 all-reduce.8.cloned.1.call-start
  446.2 122.1 %reduce-scatter.2.cloned.1.call-done = f32[64,1024]{1,0:T(8,128)} async-done(((f32[1024,1024]{1,0:T(8,128)}), f32[64,1024]{1,0:T(8,128)}) %reduce-scatter.2.cloned.1.call-update) | async-done | bytes 262160 | tf_op jit(solution)/shard_map/reduce_scatter | solution.py:80
  568.2 0.0 all-reduce.8.cloned.1.call-update
  568.3 562.0 %all-reduce.8.cloned.1.call-done = f32[64,1024]{1,0:T(8,128)} async-done(((f32[64,1024]{1,0:T(8,128)}), f32[64,1024]{1,0:T(8,128)}) %all-reduce.8.cloned.1.call-update) | async-done | bytes 262160 | tf_op jit(solution)/shard_map/psum | solution.py:81
  1130.3 1.7 copy.19
  (8 shorter events, 0.1 us)
Async XLA Ops:
  7.2 249.8 %all-gather.3.cloned.1.call-start = ((), (), s32[]{:S(2)}) async-start(), calls=%async_computation.3 | async-start | bytes 8650752 | tf_op jit(solution)/shard_map/all_gather | solution.py:54
  8.9 559.3 %reduce-scatter.2.cloned.1.call-start = ((), (), s32[]{:S(2)}) async-start(), calls=%async_computation.1 | async-start | bytes 4456448 | tf_op jit(solution)/shard_map/reduce_scatter | solution.py:80
  256.9 4.6 copy-start.2
  256.9 16.3 %copy-start = (f32[8,32,128]{2,1,0:T(8,128)S(1)}, f32[8,32,128]{2,1,0:T(8,128)}, u32[]{:S(2)}) copy-start(f32[8,32,128]{2,1,0:T(8,128)} %param.10) | copy-start | bytes 393220
  262.3 10.0 collective-permute-start
  266.5 6.7 collective-permute-start.1
  273.5 10.5 collective-permute-start.2
  275.8 9.1 collective-permute-start.3
  285.3 6.4 collective-permute-start.4
  289.9 6.7 collective-permute-start.5
  296.9 143.6 %collective-permute-start.6 = (f32[1,32,128]{2,1,0:T(8,128)S(1)}, f32[1,32,128]{2,1,0:T(8,128)S(1)}, u32[]{:S(2)}, u32[]{:S(2)}) collective-permute-start(f32[1,32,128]{2,1,0:T(8,128)S(1)} %get-tuple-element.16), channel_id=1, source_target_pairs={{1,0},{2,1},{3,2},{4,3},{5,4},{6,5},{7,6},{8,7},{9,8},{10,9},{11,1... | collective-permute-start | bytes 49160 | tf_op jit(solution)/shard_map/ppermute | solution.py:19
  298.8 141.7 %collective-permute-start.7 = (f32[1,32,128]{2,1,0:T(8,128)S(1)}, f32[1,32,128]{2,1,0:T(8,128)S(1)}, u32[]{:S(2)}, u32[]{:S(2)}) collective-permute-start(f32[1,32,128]{2,1,0:T(8,128)S(1)} %get-tuple-element.15), channel_id=1, source_target_pairs={{0,1},{1,2},{2,3},{3,4},{4,5},{5,6},{6,7},{7,8},{8,9},{9,10},{10,1... | collective-permute-start | bytes 49160 | tf_op jit(solution)/shard_map/ppermute | solution.py:16
  441.0 5.1 copy-start.1
  446.1 684.2 %all-reduce.8.cloned.1.call-start = ((), (), s32[]{:S(2)}) async-start(), calls=%async_computation.2 | async-start | bytes 524288 | tf_op jit(solution)/shard_map/psum | solution.py:81
Sparse Core Ops, SparseCore 0:
  12.9 244.0 all-gather.2
  446.2 121.9 reduce-scatter.1
  571.1 559.1 all-reduce.7
where the time goes:
time: 1160 us; the launch traced here: 1140 us
  waiting for transfers between devices  934 us (81%)
  blocking collectives  137 us (12%)
  starting transfers between devices  32.6 us (3%)
  between operations  16.6 us (1%)
    psum x1, waiting for transfers between devices, local(): moments = lax.psum(partial_rows, 'grp')  562 us
    all_gather x1, waiting for transfers between devices, local(): pieces = lax.all_gather(bundle[None], 'grp', axis=0, tiled=True)  243 us
    psum x1, blocking collectives, local(): weight_sum = lax.psum(jnp.sum(weights), 'grp')  137 us
    reduce_scatter x1, waiting for transfers between devices, local(): lax.psum_scatter(share * product, 'tile', scatter_dimension=0, tiled=True)  122 us
  transfers between devices with their start and end apart: 11, of which 6 were waited for; matrix products, arithmetic and copies ran while one was open for 0% of the time, Pallas kernels for 0%

commit v1 on v0

v1 whole, which is shorter than its diff:
```python
import jax
import jax.numpy as jnp
from jax import lax
from jax.experimental import pallas as pl
from jax.experimental.pallas import tpu as pltpu
from jax.sharding import PartitionSpec as P

MESH = pl.DeviceIdType.MESH
F32 = jnp.float32
BF16 = jnp.bfloat16
CHUNKS = 2
HALO = 4


def device(x, y, z, core):
    return {"grp": (x * 4 + y) * 2 + z // 8, "tile": (z % 8) * 2 + core}


def split(value):
    high = value.astype(BF16)
    return high, (value - high.astype(F32)).astype(BF16)


def shifted(value, axis, fill):
    size = value.shape[axis]
    place = lax.broadcasted_iota(jnp.int32, value.shape, axis)
    up = jnp.where(place == 0, fill, pltpu.roll(value, 1, axis))
    down = jnp.where(place == size - 1, fill, pltpu.roll(value, size - 1, axis))
    return up + down


def kernel(
    log_cond, potential, noise, source, parents, accept, weights,
    cond_out, pot_out, mom_out,
    gathered, sent, picked, zsent, zgot, halo, field, prop, kcon, inv, once,
    perm, rows, cols, partial, corner, summed, zsum, wbuf,
    send_gather, recv_gather, send_pick, recv_pick, send_z, recv_z, send_halo, recv_halo,
    send_rows, recv_rows, send_core, recv_core, send_sum, recv_sum, send_all, recv_all, send_w, recv_w,
):
    group, tile = lax.axis_index("grp"), lax.axis_index("tile")
    x, y, z = group // 8, (group // 2) % 4, (group % 2) * 8 + tile // 2
    high_z, core = group % 2, tile % 2
    pending = {}

    def copy(src, dst, sends, recvs, target):
        made = pltpu.make_async_remote_copy(
            src_ref=src, dst_ref=dst, send_sem=sends, recv_sem=recvs, device_id=target, device_id_type=MESH
        )
        made.start()
        pending[id(made)] = made
        return made

    def drain(copies):
        for made in copies:
            made.wait_send()
            del pending[id(made)]

    def along(axis, d):
        if axis == 0:
            return device((x + d) % 4, y, z, core)
        return device(x, (y + d) % 4, z, core)

    beyond = device(x, y, (z + 15 + 2 * core) % 16, 1 - core)
    partner = device(x, y, z, 1 - core)
    below = {"grp": (x * 4 + y) * 2 + ((z * 2 + core + 31) % 32) // 16, "tile": (tile + 15) % 16}
    above = {"grp": (x * 4 + y) * 2 + ((z * 2 + core + 1) % 32) // 16, "tile": (tile + 1) % 16}

    barrier = pltpu.get_barrier_semaphore()
    greeted = [device((x + a) % 4, (y + b) % 4, z, core) for a in range(4) for b in range(4) if a or b]
    greeted += [device(x, y, (z + d) % 16, core) for d in range(1, 16)]
    greeted += [beyond, partner]
    for other in greeted:
        pl.semaphore_signal(barrier, inc=1, device_id=other, device_id_type=MESH)
    pl.semaphore_wait(barrier, len(greeted))

    fields = (log_cond, potential)
    planes = 8 // CHUNKS
    chunk = [pl.ds(k * planes, planes) for k in range(CHUNKS)]
    gathers = {}
    for k in range(CHUNKS):
        for f in range(2):
            for d in range(1, 4):
                at = (f * CHUNKS + k) * 3 + d - 1
                gathers[f, k, d] = copy(
                    fields[f].at[chunk[k]], gathered[f][k].at[d], send_gather.at[at], recv_gather.at[at], along(f, d)
                )

    halos = []
    parts = ((noise.at[0], 0, 4), (noise.at[1], 4, 2), (source, 6, 3))
    for i, (ref, start, width) in enumerate(parts):
        halos.append(copy(ref.at[pl.ds(0, width)], halo.at[1, pl.ds(start, width)], send_halo.at[i], recv_halo.at[i], below))
        halos.append(
            copy(ref.at[pl.ds(8 - width, width)], halo.at[0, pl.ds(start, width)], send_halo.at[3 + i], recv_halo.at[3 + i], above)
        )
    for f in range(2):
        for k in range(CHUNKS):
            gathered[f][k][0] = fields[f][chunk[k]]

    wvec = jnp.full((8, 128), weights[0], F32)
    wbuf[0, 0] = wvec
    wcopies = [copy(wbuf.at[0, 0], wbuf.at[0, d], send_w.at[d - 1], recv_w.at[d - 1], along(0, d)) for d in range(1, 4)]

    def parent(a, b, c):
        return parents[(a * 4 + b) * 2 + c]

    def coordinate(p, axis):
        return p // 8 if axis == 0 else (p // 2) % 4

    mine = (x, y)
    picks = {}

    def spread(f, k, kind):
        first, second = f, 1 - f
        to_z = high_z if kind == 0 else 1 - high_z
        for d in (1, 2, 3, 0):
            p = parent((x + d) % 4, y, to_z) if second == 0 else parent(x, (y + d) % 4, to_z)
            slot = (mine[first] - coordinate(p, first) + 4) % 4
            block = gathered[f][k][slot]
            if d == 0:
                picked[f][kind][k][0] = block
            else:
                sent[f, kind, d - 1, chunk[k]] = block
                at = ((f * 2 + kind) * CHUNKS + k) * 3 + d - 1
                picks[f, kind, k, d] = copy(
                    sent.at[f, kind, d - 1, chunk[k]], picked[f][kind][k].at[d], send_pick.at[at], recv_pick.at[at], along(second, d)
                )

    def choose(f, k, kind):
        second = 1 - f
        for d in range(1, 4):
            picks[f, kind, k, d].wait_recv()
        p = parent(x, y, high_z if kind == 0 else 1 - high_z)
        return picked[f][kind][k][(mine[second] - coordinate(p, second) + 4) % 4]

    for k in range(CHUNKS):
        for f in range(2):
            for d in range(1, 4):
                gathers[f, k, d].wait_recv()
            spread(f, k, 1)
    zcopies = {}
    for k in range(CHUNKS):
        for f in range(2):
            zsent[f, chunk[k]] = choose(f, k, 1)
            at = f * CHUNKS + k
            zcopies[f, k] = copy(
                zsent.at[f, chunk[k]], zgot.at[f, chunk[k]], send_z.at[at], recv_z.at[at], device(x, y, (z + 8) % 16, core)
            )
    for k in range(CHUNKS):
        for f in range(2):
            spread(f, k, 0)

    for c in wcopies:
        c.wait_recv()
    wbuf[1, 0] = wbuf[0, 0] + wbuf[0, 1] + wbuf[0, 2] + wbuf[0, 3]
    wcopies = [copy(wbuf.at[1, 0], wbuf.at[1, d], send_w.at[2 + d], recv_w.at[2 + d], along(1, d)) for d in range(1, 4)]

    from_here = jnp.full((1, 32, 128), (parent(x, y, high_z) % 2 == high_z).astype(jnp.int32)) > 0
    interior = pl.ds(HALO, 8)
    for k in range(CHUNKS):
        for f in range(2):
            own = choose(f, k, 0)
            zcopies[f, k].wait_recv()
            field[f, pl.ds(HALO + k * planes, planes)] = jnp.where(from_here, own, zgot[f, chunk[k]])

    edges = []
    for f in range(2):
        edges.append(
            copy(field.at[f, pl.ds(HALO, HALO)], field.at[f, pl.ds(HALO + 8, HALO)], send_halo.at[6 + f], recv_halo.at[6 + f], below)
        )
        edges.append(copy(field.at[f, pl.ds(8, HALO)], field.at[f, pl.ds(0, HALO)], send_halo.at[8 + f], recv_halo.at[8 + f], above))

    for c in wcopies:
        c.wait_recv()
    wbuf[2, 0] = wbuf[1, 0] + wbuf[1, 1] + wbuf[1, 2] + wbuf[1, 3]
    wlast = copy(wbuf.at[2, 0], wbuf.at[2, 1], send_w.at[6], recv_w.at[6], device(x, y, (z + 8) % 16, core))

    for c in halos + edges:
        c.wait_recv()

    has_below = jnp.full((32, 128), (tile > 0).astype(jnp.int32))
    has_above = jnp.full((32, 128), (tile < 15).astype(jnp.int32))

    def inside(i, value):
        if i < HALO:
            return jnp.where(has_below > 0, value, 0.0)
        if i >= HALO + 8:
            return jnp.where(has_above > 0, value, 0.0)
        return value

    for f in range(2):
        for i in (*range(HALO), *range(HALO + 8, 2 * HALO + 8)):
            field[f, i] = inside(i, field[f, i])

    def border(ref, start, width, i):
        if i < HALO:
            return halo[0, start + width - HALO + i]
        if i >= HALO + 8:
            return halo[1, start + i - HALO - 8]
        return ref[i - HALO]

    def sweep(i, v_at):
        here, low, up = v_at(i), v_at(i - 1), v_at(i + 1)
        k = kcon[i]
        kv = k * here
        near = low + up + shifted(here, 0, 0.0) + shifted(here, 1, 0.0)
        weighted = kcon[i - 1] * low + kcon[i + 1] * up + shifted(kv, 0, 0.0) + shifted(kv, 1, 0.0)
        return k, near, weighted, here

    for m in range(2):
        edge = 2 * m
        last = 2 * HALO + 8 - edge
        for i in range(edge, last):
            fresh = border(noise.at[m], 0 if m == 0 else 4, 4 if m == 0 else 2, i)
            value = inside(i, 0.8 * field[0, i] + 0.6 * fresh)
            prop[i] = value
            kcon[i] = jnp.exp(value)
        flag = jnp.full((32, 128), accept[m, 0]) > 0
        for i in range(edge + 1, last - 1):
            k, near, weighted, here = sweep(i, lambda j: field[1, j])
            inv[i] = 0.8 / (6.0 * k + kcon[i - 1] + kcon[i + 1] + shifted(k, 0, 1.0) + shifted(k, 1, 1.0))
            value = 0.2 * here + (2.0 * border(source, 6, 3, i) + k * near + weighted) * inv[i]
            once[i] = inside(i, value)
        if m == 0:
            drain(edges)
        for i in range(edge + 2, last - 2):
            k, near, weighted, here = sweep(i, lambda j: once[j])
            value = 0.2 * here + (2.0 * border(source, 6, 3, i) + k * near + weighted) * inv[i]
            field[0, i] = jnp.where(flag, prop[i], field[0, i])
            field[1, i] = jnp.where(flag, inside(i, value), field[1, i])

    final = field[1, interior]
    cond_out[...] = field[0, interior]
    pot_out[...] = final

    columns = [
        copy(field.at[1, pl.ds(HALO + 2 * ((y + d) % 4), 2)], cols.at[0, d], send_rows.at[d - 1], recv_rows.at[d - 1], along(1, d))
        for d in range(1, 4)
    ]
    cols[0, 0] = field[1, pl.ds(HALO + 2 * y, 2)]
    scaled = final * weights[0]
    into = lax.broadcasted_iota(jnp.int32, (512, 512), 0)
    out = lax.broadcasted_iota(jnp.int32, (512, 512), 1)
    wanted = ((out // 16) % 4) * 128 + ((out // 64) % 2) * 64 + (out // 128) * 16 + out % 16
    select = jnp.where(into == wanted, 1.0, 0.0).astype(BF16)
    stacked = jnp.concatenate(
        [jnp.concatenate([scaled[4 * half + j] for j in range(4)], axis=1) for half in range(2)], axis=0
    )
    high, low = split(stacked)
    shuffled = jnp.dot(high, select, preferred_element_type=F32) + jnp.dot(low, select, preferred_element_type=F32)
    for j in range(4):
        for half in range(2):
            perm[j, half] = shuffled[32 * half : 32 * half + 32, 128 * j : 128 * j + 128]
    taken = [
        copy(perm.at[(x + d) % 4], rows.at[0, d], send_rows.at[2 + d], recv_rows.at[2 + d], along(0, d)) for d in range(1, 4)
    ]
    rows[0, 0] = perm[x]
    for c in columns:
        c.wait_recv()
    columns = [copy(cols.at[0], cols.at[d], send_rows.at[5 + d], recv_rows.at[5 + d], along(0, d)) for d in range(1, 4)]
    for c in taken:
        c.wait_recv()
    taken = [copy(rows.at[0], rows.at[d], send_rows.at[8 + d], recv_rows.at[8 + d], along(1, d)) for d in range(1, 4)]
    for c in columns + taken:
        c.wait_recv()

    right = jnp.concatenate(
        [jnp.concatenate([cols[dx, dy, 0], cols[dx, dy, 1]], axis=1) for dy in range(4) for dx in range(4)], axis=0
    )
    right_high, right_low = split(right)
    for half in range(2):
        left = jnp.concatenate([rows[dy, dx, half] for dy in range(4) for dx in range(4)], axis=0).T
        left_high, left_low = split(left)
        product = (
            jnp.dot(left_high, right_high, preferred_element_type=F32)
            + jnp.dot(left_high, right_low, preferred_element_type=F32)
            + jnp.dot(left_low, right_high, preferred_element_type=F32)
        )
        for c in range(2):
            partial[c, half] = product[64 * c : 64 * c + 64]
    swapped = copy(partial.at[1 - core], corner, send_core, recv_core, partner)
    swapped.wait_recv()
    for half in range(2):
        total = partial[core, half] + corner[half]
        for j in range(4):
            summed[4 * half + j] = total[16 * j : 16 * j + 16]
    sums = [
        copy(summed.at[(z + d) % 8], zsum.at[d], send_sum.at[d], recv_sum.at[d], device(x, y, (z + d) % 16, core))
        for d in range(1, 16)
    ]
    wlast.wait_recv()
    for c in sums:
        c.wait_recv()
    total = summed[z % 8]
    for d in range(1, 16):
        total = total + zsum[d]
    weight_sum = wbuf[2, 0] + wbuf[2, 1]
    mom_out[x, y] = total / weight_sum[0:1, 0:1]
    others = [(a, b) for a in range(4) for b in range(4) if a or b]
    last = [
        copy(
            mom_out.at[x, y], mom_out.at[x, y], send_all.at[i], recv_all.at[i], device((x + a) % 4, (y + b) % 4, z, core)
        )
        for i, (a, b) in enumerate(others)
    ]
    for c in last:
        c.wait_recv()
    for c in pending.values():
        c.wait_send()


def local(log_cond, potential, noise, source, parents, accept, weights):
    vmem, smem = pl.BlockSpec(memory_space=pltpu.VMEM), pl.BlockSpec(memory_space=pltpu.SMEM)
    dma = pltpu.SemaphoreType.DMA
    block = (8, 32, 128)
    four = (4, 8 // CHUNKS, 32, 128)
    wide = (2 * HALO + 8, 32, 128)
    conduct, pot, moments = pl.pallas_call(
        kernel,
        out_shape=(
            jax.ShapeDtypeStruct(block, F32),
            jax.ShapeDtypeStruct(block, F32),
            jax.ShapeDtypeStruct((4, 4, 16, 256), F32),
        ),
        in_specs=[vmem, vmem, vmem, vmem, smem, smem, smem],
        out_specs=(vmem, vmem, vmem),
        scratch_shapes=[
            ((pltpu.VMEM(four, F32),) * CHUNKS,) * 2,
            pltpu.VMEM((2, 2, 3, *block), F32),
            (((pltpu.VMEM(four, F32),) * CHUNKS,) * 2,) * 2,
            pltpu.VMEM((2, *block), F32),
            pltpu.VMEM((2, *block), F32),
            pltpu.VMEM((2, 9, 32, 128), F32),
            pltpu.VMEM((2, *wide), F32),
            pltpu.VMEM(wide, F32),
            pltpu.VMEM(wide, F32),
            pltpu.VMEM(wide, F32),
            pltpu.VMEM(wide, F32),
            pltpu.VMEM((4, 2, 32, 128), F32),
            pltpu.VMEM((4, 4, 2, 32, 128), F32),
            pltpu.VMEM((4, 4, 2, 32, 128), F32),
            pltpu.VMEM((2, 2, 64, 256), F32),
            pltpu.VMEM((2, 64, 256), F32),
            pltpu.VMEM((8, 16, 256), F32),
            pltpu.VMEM((16, 16, 256), F32),
            pltpu.VMEM((3, 4, 8, 128), F32),
            dma((6 * CHUNKS,)), dma((6 * CHUNKS,)),
            dma((12 * CHUNKS,)), dma((12 * CHUNKS,)),
            dma((2 * CHUNKS,)), dma((2 * CHUNKS,)),
            dma((10,)), dma((10,)),
            dma((12,)), dma((12,)),
            dma, dma,
            dma((16,)), dma((16,)),
            dma((15,)), dma((15,)),
            dma((7,)), dma((7,)),
        ],
        compiler_params=pltpu.CompilerParams(collective_id=0, has_side_effects=True),
        name="resample_move",
    )(log_cond[0], potential[0], noise[:, 0], source, parents, accept, weights)
    return conduct[None], pot[None], moments.transpose(0, 2, 1, 3).reshape(64, 1024)


def solution(mesh):
    placed = (
        P("grp", "tile", None, None),
        P("grp", "tile", None, None),
        P(None, "grp", "tile", None, None),
        P("tile", None, None),
        P(),
        P(None, "grp"),
        P("grp"),
    )
    return jax.shard_map(
        local,
        mesh=mesh,
        in_specs=placed,
        out_specs=(P("grp", "tile", None, None), P("grp", "tile", None, None), P("tile", None)),
        check_vma=False,
    )
```

time: 1160 us -> 106 us (0.09); the launches traced: 1140 us -> 106 us
  waiting for transfers between devices: 934 us -> 0 us
  blocking collectives: 137 us -> 0 us
  Pallas kernels: 0 us -> 99.3 us
  starting transfers between devices: 32.6 us -> 0 us
  between operations: 16.6 us -> 1.31 us
    psum x1 -> x0, waiting for transfers between devices: 562 us -> none  [local(): moments = lax.psum(partial_rows, 'grp')]
    all_gather x1 -> x0, waiting for transfers between devices: 243 us -> none  [local(): pieces = lax.all_gather(bundle[None], 'grp', axis=0, tiled=True)]
    psum x1 -> x0, blocking collectives: 137 us -> none  [local(): weight_sum = lax.psum(jnp.sum(weights), 'grp')]
    reduce_scatter x1 -> x0, waiting for transfers between devices: 122 us -> none  [local(): lax.psum_scatter(share * product, 'tile', scatter_dimension=0, tiled=True)]
    pallas_call x0 -> x1, Pallas kernels: none -> 99.3 us  [local(): pl.pallas_call(kernel, out_shape=(jax.ShapeDtypeStruct(block, F32), jax.S...]
    ppermute x8 -> x0, starting transfers between devices: 32.5 us -> none  [the longest x4 20.5 us: with_halo(): lax.ppermute(lax.slice_in_dim(block, block.shape[dim] - width, None, axis...]
  transfers between devices with their start and end apart: 11 -> 0, of which waited for: 6 -> 0; matrix products, arithmetic and copies ran while one was open for 0% -> 0% of each run, Pallas kernels for 0% -> 0%
where the time goes in v1:
time: 106 us
  Pallas kernels  99.3 us (94%)
  local copies, waits for them, and re-layouts  4.92 us (5%)
  between operations  1.31 us (1%)
    pallas_call x1, Pallas kernels, local(): pl.pallas_call(kernel, out_shape=(jax.ShapeDtypeStruct(block, F32), jax.S...  99.3 us
    unnamed x10, local copies, waits for them, and re-layouts  3.8 us

profile of v1, /device:TPU:1, one launch (start us, length us, event | category | flops | bytes accessed | tf_op | source)
XLA Modules:
  0.0 105.6 jit_solution(9052261637027937723)
XLA Ops:
  1.3 0.0 copy-start.2
  1.3 0.6 copy-done.2
  1.9 0.6 copy.11.accept
  2.6 99.3 %resample_move.1 = (f32[8,32,128]{2,1,0:T(8,128)}, f32[8,32,128]{2,1,0:T(8,128)}, f32[4,4,16,256]{3,2,1,0:T(8,128)}) custom-call(f32[8,32,128]{2,1,0:T(8,128)} %bitcast.13, f32[8,32,128]{2,1,0:T(8,128)} %bitcast.14, f32[2,8,32,128]{3,2,1,0:T(8,128)} %bitcast.10, f32[8,32,128]{2,1,0:T(8,128)} %source.1, s32[32]{0:T(128)} %parents.1, s32[2,1]{1,0:T(2,128)} %copy.11.accept, ...), custom_call_target="tpu_custom_call" | custom-call | tf_op jit(solution)/shard_map/resample_move/pallas_call | solution.py:317
  101.9 1.1 %copy.12 = f32[4,16,4,256]{3,2,1,0:T(4,128)S(1)} copy(f32[4,16,4,256]{3,1,2,0:T(8,128)} %bitcast.12) | data formatting | bytes 524288 | tf_op jit(solution)/shard_map/transpose | solution.py:359
  103.0 0.0 copy-start.1
  103.0 0.8 copy.13
  103.8 0.1 copy-done.1
  103.9 0.0 copy-start
  103.9 0.7 copy.17
  104.6 0.3 copy-done
  104.9 0.7 copy.18
Async XLA Ops:
  1.3 0.7 copy-start.2
  103.0 0.9 copy-start.1
  103.9 1.0 copy-start

commit v2 on v1

--- a/solution.py
+++ b/solution.py
@@ -8,7 +8,7 @@
 MESH = pl.DeviceIdType.MESH
 F32 = jnp.float32
 BF16 = jnp.bfloat16
-CHUNKS = 2
+CHUNKS = 4
 HALO = 4
 
 
@@ -32,9 +32,9 @@
 def kernel(
     log_cond, potential, noise, source, parents, accept, weights,
     cond_out, pot_out, mom_out,
-    gathered, sent, picked, zsent, zgot, halo, field, prop, kcon, inv, once,
+    pot_got, cond_got, sent, picked, zsent, zgot, halo, field, prop, kcon, inv, once,
     perm, rows, cols, partial, corner, summed, zsum, wbuf,
-    send_gather, recv_gather, send_pick, recv_pick, send_z, recv_z, send_halo, recv_halo,
+    send_gather, recv_gather, send_pick, recv_pick, send_z, recv_z, send_halo, recv_halo, send_edge, recv_edge,
     send_rows, recv_rows, send_core, recv_core, send_sum, recv_sum, send_all, recv_all, send_w, recv_w,
 ):
     group, tile = lax.axis_index("grp"), lax.axis_index("tile")
@@ -73,17 +73,22 @@
         pl.semaphore_signal(barrier, inc=1, device_id=other, device_id_type=MESH)
     pl.semaphore_wait(barrier, len(greeted))
 
-    fields = (log_cond, potential)
+    across = device(x, y, (z + 8) % 16, core)
     planes = 8 // CHUNKS
     chunk = [pl.ds(k * planes, planes) for k in range(CHUNKS)]
-    gathers = {}
-    for k in range(CHUNKS):
-        for f in range(2):
-            for d in range(1, 4):
-                at = (f * CHUNKS + k) * 3 + d - 1
-                gathers[f, k, d] = copy(
-                    fields[f].at[chunk[k]], gathered[f][k].at[d], send_gather.at[at], recv_gather.at[at], along(f, d)
-                )
+    chunks = range(CHUNKS)
+    zcond = [
+        copy(log_cond.at[chunk[k]], cond_got[k].at[4], send_z.at[k], recv_z.at[k], across) for k in chunks
+    ]
+
+    def gather(src, dst, k, kind):
+        made = []
+        for d in range(1, 4):
+            at = (kind * CHUNKS + k) * 3 + d - 1
+            made.append(copy(src, dst(d), send_gather.at[at], recv_gather.at[at], along(0, d)))
+        return made
+
+    pot_near = [gather(potential.at[chunk[k]], lambda d: pot_got[k].at[d], k, 0) for k in chunks]
 
     halos = []
     parts = ((noise.at[0], 0, 4), (noise.at[1], 4, 2), (source, 6, 3))
@@ -92,9 +97,10 @@
         halos.append(
             copy(ref.at[pl.ds(8 - width, width)], halo.at[0, pl.ds(start, width)], send_halo.at[3 + i], recv_halo.at[3 + i], above)
         )
-    for f in range(2):
-        for k in range(CHUNKS):
-            gathered[f][k][0] = fields[f][chunk[k]]
+    cond_near = [gather(log_cond.at[chunk[k]], lambda d: cond_got[k].at[d], k, 1) for k in chunks]
+    for k in chunks:
+        pot_got[k][0] = potential[chunk[k]]
+        cond_got[k][0] = log_cond[chunk[k]]
 
     wvec = jnp.full((8, 128), weights[0], F32)
     wbuf[0, 0] = wvec
@@ -103,76 +109,81 @@
     def parent(a, b, c):
         return parents[(a * 4 + b) * 2 + c]
 
-    def coordinate(p, axis):
-        return p // 8 if axis == 0 else (p // 2) % 4
-
-    mine = (x, y)
     picks = {}
 
-    def spread(f, k, kind):
-        first, second = f, 1 - f
-        to_z = high_z if kind == 0 else 1 - high_z
-        for d in (1, 2, 3, 0):
-            p = parent((x + d) % 4, y, to_z) if second == 0 else parent(x, (y + d) % 4, to_z)
-            slot = (mine[first] - coordinate(p, first) + 4) % 4
-            block = gathered[f][k][slot]
+    def spread(k, kind):
+        to_z = 1 - high_z if kind == 1 else high_z
+        for d in (2, 1, 3, 0):
+            p = parent(x, (y + d) % 4, to_z)
+            slot = (x - p // 8 + 4) % 4
+            if kind == 2:
+                block = cond_got[k][((p + high_z) % 2) * 4 + slot]
+            else:
+                block = pot_got[k][slot]
             if d == 0:
-                picked[f][kind][k][0] = block
+                picked[kind][k][0] = block
             else:
-                sent[f, kind, d - 1, chunk[k]] = block
-                at = ((f * 2 + kind) * CHUNKS + k) * 3 + d - 1
-                picks[f, kind, k, d] = copy(
-                    sent.at[f, kind, d - 1, chunk[k]], picked[f][kind][k].at[d], send_pick.at[at], recv_pick.at[at], along(second, d)
+                sent[kind, k, d - 1] = block
+                at = (kind * CHUNKS + k) * 3 + d - 1
+                picks[kind, k, d] = copy(
+                    sent.at[kind, k, d - 1], picked[kind][k].at[d], send_pick.at[at], recv_pick.at[at], along(1, d)
                 )
 
-    def choose(f, k, kind):
-        second = 1 - f
+    def choose(k, kind):
         for d in range(1, 4):
-            picks[f, kind, k, d].wait_recv()
-        p = parent(x, y, high_z if kind == 0 else 1 - high_z)
-        return picked[f][kind][k][(mine[second] - coordinate(p, second) + 4) % 4]
-
-    for k in range(CHUNKS):
-        for f in range(2):
-            for d in range(1, 4):
-                gathers[f, k, d].wait_recv()
-            spread(f, k, 1)
-    zcopies = {}
-    for k in range(CHUNKS):
-        for f in range(2):
-            zsent[f, chunk[k]] = choose(f, k, 1)
-            at = f * CHUNKS + k
-            zcopies[f, k] = copy(
-                zsent.at[f, chunk[k]], zgot.at[f, chunk[k]], send_z.at[at], recv_z.at[at], device(x, y, (z + 8) % 16, core)
-            )
-    for k in range(CHUNKS):
-        for f in range(2):
-            spread(f, k, 0)
+            picks[kind, k, d].wait_recv()
+        p = parent(x, y, 1 - high_z if kind == 1 else high_z)
+        return picked[kind][k][(y - (p // 2) % 4 + 4) % 4]
+
+    for k in chunks:
+        for c in pot_near[k]:
+            c.wait_recv()
+        spread(k, 1)
+    zpot = []
+    for k in chunks:
+        zsent[k] = choose(k, 1)
+        zpot.append(copy(zsent.at[k], zgot.at[k], send_z.at[CHUNKS + k], recv_z.at[CHUNKS + k], across))
+    for k in chunks:
+        spread(k, 0)
+    cond_far = []
+    for k in chunks:
+        zcond[k].wait_recv()
+        cond_far.append(gather(cond_got[k].at[4], lambda d: cond_got[k].at[4 + d], k, 2))
 
     for c in wcopies:
         c.wait_recv()
     wbuf[1, 0] = wbuf[0, 0] + wbuf[0, 1] + wbuf[0, 2] + wbuf[0, 3]
     wcopies = [copy(wbuf.at[1, 0], wbuf.at[1, d], send_w.at[2 + d], recv_w.at[2 + d], along(1, d)) for d in range(1, 4)]
 
+    for k in chunks:
+        for c in cond_near[k] + cond_far[k]:
+            c.wait_recv()
+        spread(k, 2)
+
     from_here = jnp.full((1, 32, 128), (parent(x, y, high_z) % 2 == high_z).astype(jnp.int32)) > 0
     interior = pl.ds(HALO, 8)
-    for k in range(CHUNKS):
-        for f in range(2):
-            own = choose(f, k, 0)
-            zcopies[f, k].wait_recv()
-            field[f, pl.ds(HALO + k * planes, planes)] = jnp.where(from_here, own, zgot[f, chunk[k]])
-
     edges = []
-    for f in range(2):
-        edges.append(
-            copy(field.at[f, pl.ds(HALO, HALO)], field.at[f, pl.ds(HALO + 8, HALO)], send_halo.at[6 + f], recv_halo.at[6 + f], below)
-        )
-        edges.append(copy(field.at[f, pl.ds(8, HALO)], field.at[f, pl.ds(0, HALO)], send_halo.at[8 + f], recv_halo.at[8 + f], above))
+
+    def place(f, k, value):
+        start = k * planes
+        field[f, pl.ds(HALO + start, planes)] = value
+        src, at = field.at[f, pl.ds(HALO + start, planes)], f * CHUNKS + k
+        if start < HALO:
+            edges.append(copy(src, field.at[f, pl.ds(HALO + 8 + start, planes)], send_edge.at[at], recv_edge.at[at], below))
+        else:
+            edges.append(copy(src, field.at[f, pl.ds(start - HALO, planes)], send_edge.at[at], recv_edge.at[at], above))
+
+    for k in chunks:
+        place(0, k, choose(k, 2))
+    for k in chunks:
+        own = choose(k, 0)
+        zpot[k].wait_recv()
+        place(1, k, jnp.where(from_here, own, zgot[k]))
 
     for c in wcopies:
         c.wait_recv()
     wbuf[2, 0] = wbuf[1, 0] + wbuf[1, 1] + wbuf[1, 2] + wbuf[1, 3]
-    wlast = copy(wbuf.at[2, 0], wbuf.at[2, 1], send_w.at[6], recv_w.at[6], device(x, y, (z + 8) % 16, core))
+    wlast = copy(wbuf.at[2, 0], wbuf.at[2, 1], send_w.at[6], recv_w.at[6], across)
 
     for c in halos + edges:
         c.wait_recv()
@@ -214,7 +225,7 @@
             value = inside(i, 0.8 * field[0, i] + 0.6 * fresh)
             prop[i] = value
             kcon[i] = jnp.exp(value)
-        flag = jnp.full((32, 128), accept[m, 0]) > 0
+        flag = jnp.full((32, 128), accept[m]) > 0
         for i in range(edge + 1, last - 1):
             k, near, weighted, here = sweep(i, lambda j: field[1, j])
             inv[i] = 0.8 / (6.0 * k + kcon[i - 1] + kcon[i + 1] + shifted(k, 0, 1.0) + shifted(k, 1, 1.0))
@@ -285,7 +296,7 @@
             summed[4 * half + j] = total[16 * j : 16 * j + 16]
     sums = [
         copy(summed.at[(z + d) % 8], zsum.at[d], send_sum.at[d], recv_sum.at[d], device(x, y, (z + d) % 16, core))
-        for d in range(1, 16)
+        for d in sorted(range(1, 16), key=lambda d: -min(d, 16 - d))
     ]
     wlast.wait_recv()
     for c in sums:
@@ -294,11 +305,12 @@
     for d in range(1, 16):
         total = total + zsum[d]
     weight_sum = wbuf[2, 0] + wbuf[2, 1]
-    mom_out[x, y] = total / weight_sum[0:1, 0:1]
+    piece = mom_out.at[pl.ds(pl.multiple_of(x * 16, 16), 16), pl.ds(pl.multiple_of(y * 256, 256), 256)]
+    piece[...] = total / weight_sum[0:1, 0:1]
     others = [(a, b) for a in range(4) for b in range(4) if a or b]
     last = [
         copy(
-            mom_out.at[x, y], mom_out.at[x, y], send_all.at[i], recv_all.at[i], device((x + a) % 4, (y + b) % 4, z, core)
+            piece, piece, send_all.at[i], recv_all.at[i], device((x + a) % 4, (y + b) % 4, z, core)
         )
         for i, (a, b) in enumerate(others)
     ]
@@ -312,23 +324,24 @@
     vmem, smem = pl.BlockSpec(memory_space=pltpu.VMEM), pl.BlockSpec(memory_space=pltpu.SMEM)
     dma = pltpu.SemaphoreType.DMA
     block = (8, 32, 128)
-    four = (4, 8 // CHUNKS, 32, 128)
+    part = (8 // CHUNKS, 32, 128)
     wide = (2 * HALO + 8, 32, 128)
     conduct, pot, moments = pl.pallas_call(
         kernel,
         out_shape=(
             jax.ShapeDtypeStruct(block, F32),
             jax.ShapeDtypeStruct(block, F32),
-            jax.ShapeDtypeStruct((4, 4, 16, 256), F32),
+            jax.ShapeDtypeStruct((64, 1024), F32),
         ),
         in_specs=[vmem, vmem, vmem, vmem, smem, smem, smem],
         out_specs=(vmem, vmem, vmem),
         scratch_shapes=[
-            ((pltpu.VMEM(four, F32),) * CHUNKS,) * 2,
-            pltpu.VMEM((2, 2, 3, *block), F32),
-            (((pltpu.VMEM(four, F32),) * CHUNKS,) * 2,) * 2,
-            pltpu.VMEM((2, *block), F32),
-            pltpu.VMEM((2, *block), F32),
+            (pltpu.VMEM((4, *part), F32),) * CHUNKS,
+            (pltpu.VMEM((8, *part), F32),) * CHUNKS,
+            pltpu.VMEM((3, CHUNKS, 3, *part), F32),
+            ((pltpu.VMEM((4, *part), F32),) * CHUNKS,) * 3,
+            pltpu.VMEM((CHUNKS, *part), F32),
+            pltpu.VMEM((CHUNKS, *part), F32),
             pltpu.VMEM((2, 9, 32, 128), F32),
             pltpu.VMEM((2, *wide), F32),
             pltpu.VMEM(wide, F32),
@@ -343,10 +356,11 @@
             pltpu.VMEM((8, 16, 256), F32),
             pltpu.VMEM((16, 16, 256), F32),
             pltpu.VMEM((3, 4, 8, 128), F32),
-            dma((6 * CHUNKS,)), dma((6 * CHUNKS,)),
-            dma((12 * CHUNKS,)), dma((12 * CHUNKS,)),
+            dma((9 * CHUNKS,)), dma((9 * CHUNKS,)),
+            dma((9 * CHUNKS,)), dma((9 * CHUNKS,)),
             dma((2 * CHUNKS,)), dma((2 * CHUNKS,)),
-            dma((10,)), dma((10,)),
+            dma((6,)), dma((6,)),
+            dma((2 * CHUNKS,)), dma((2 * CHUNKS,)),
             dma((12,)), dma((12,)),
             dma, dma,
             dma((16,)), dma((16,)),
@@ -355,8 +369,8 @@
         ],
         compiler_params=pltpu.CompilerParams(collective_id=0, has_side_effects=True),
         name="resample_move",
-    )(log_cond[0], potential[0], noise[:, 0], source, parents, accept, weights)
-    return conduct[None], pot[None], moments.transpose(0, 2, 1, 3).reshape(64, 1024)
+    )(log_cond[0], potential[0], noise[:, 0], source, parents, accept.reshape(-1), weights)
+    return conduct[None], pot[None], moments
 
 
 def solution(mesh):

time: 106 us -> 91.9 us (0.87)
  Pallas kernels: 99.3 us -> 87.5 us
  local copies, waits for them, and re-layouts: 4.92 us -> 2.98 us
    pallas_call x1, Pallas kernels: 99.3 us -> 87.5 us  [local(): pl.pallas_call(kernel, out_shape=(jax.ShapeDtypeStruct(block, F32), jax.S...]
    transpose x1 -> x0, local copies, waits for them, and re-layouts: 1.12 us -> none  [local(): moments.transpose(0, 2, 1, 3).reshape(64, 1024)]
    unnamed x10 -> x7, local copies, waits for them, and re-layouts: 3.8 us -> 2.98 us
where the time goes in v2:
time: 91.9 us; the launch traced here: 91.8 us
  Pallas kernels  87.5 us (95%)
  local copies, waits for them, and re-layouts  2.98 us (3%)
  between operations  1.3 us (1%)
    pallas_call x1, Pallas kernels, local(): pl.pallas_call(kernel, out_shape=(jax.ShapeDtypeStruct(block, F32), jax.S...  87.5 us
    unnamed x7, local copies, waits for them, and re-layouts  2.98 us

profile of v2, /device:TPU:1, one launch (start us, length us, event | category | flops | bytes accessed | tf_op | source)
XLA Modules:
  0.0 91.8 jit_solution(120957249971463958)
XLA Ops:
  1.3 87.5 %resample_move.1 = (f32[8,32,128]{2,1,0:T(8,128)}, f32[8,32,128]{2,1,0:T(8,128)}, f32[64,1024]{1,0:T(8,128)}) custom-call(f32[8,32,128]{2,1,0:T(8,128)} %bitcast.9, f32[8,32,128]{2,1,0:T(8,128)} %bitcast.10, f32[2,8,32,128]{3,2,1,0:T(8,128)} %bitcast.6, f32[8,32,128]{2,1,0:T(8,128)} %source.1, s32[32]{0:T(128)} %parents.1, s32[2]{0:T(128)} %bitcast.11, ...), custom_call_target="tpu_custom_call" | custom-call | tf_op jit(solution)/shard_map/resample_move/pallas_call | solution.py:329
  88.8 0.0 copy-start.1
  88.8 0.0 copy-start
  88.8 1.6 %copy.14 = f32[1,8,32,128]{3,2,1,0:T(8,128)} copy(f32[1,8,32,128]{3,2,1,0:T(8,128)} %bitcast.8) | data formatting | bytes 262144
  90.4 0.0 copy-done.1
  90.4 0.7 copy.15
  91.1 0.0 copy-done
  91.1 0.7 copy.16
Async XLA Ops:
  88.8 1.6 %copy-start.1 = (f32[8,32,128]{2,1,0:T(8,128)S(1)}, f32[8,32,128]{2,1,0:T(8,128)}, u32[]{:S(2)}) copy-start(f32[8,32,128]{2,1,0:T(8,128)} %get-tuple-element.7) | copy-start | bytes 393220
  88.8 2.3 %copy-start = (f32[64,1024]{1,0:T(8,128)S(1)}, f32[64,1024]{1,0:T(8,128)}, u32[]{:S(2)}) copy-start(f32[64,1024]{1,0:T(8,128)} %get-tuple-element.14) | copy-start | bytes 786436

commit v3 on v2

v3 whole, which is shorter than its diff:
```python
import jax
import jax.numpy as jnp
from jax import lax
from jax.experimental import pallas as pl
from jax.experimental.pallas import tpu as pltpu
from jax.sharding import PartitionSpec as P

MESH = pl.DeviceIdType.MESH
F32 = jnp.float32
BF16 = jnp.bfloat16
CHUNKS = 4
HALO = 4


def device(x, y, z, core):
    return {"grp": (x * 4 + y) * 2 + z // 8, "tile": (z % 8) * 2 + core}


def split(value):
    high = value.astype(BF16)
    return high, (value - high.astype(F32)).astype(BF16)


def shifted(value, axis, fill):
    size = value.shape[axis]
    place = lax.broadcasted_iota(jnp.int32, value.shape, axis)
    up = jnp.where(place == 0, fill, pltpu.roll(value, 1, axis))
    down = jnp.where(place == size - 1, fill, pltpu.roll(value, size - 1, axis))
    return up + down


def kernel(
    log_cond, potential, noise_in, source_in, parents, accept, weights,
    cond_out, pot_out, mom_out,
    pot_got, cond_got, sent, picked, zsent, zgot, halo, field, prop, kcon, inv, once,
    noise, source, perm, rows, cols, partial, corner, summed, zsum, wbuf,
    send_sem, recv_gather, recv_pick, recv_z, recv_rows, recv_sem, local_sem,
):
    group, tile = lax.axis_index("grp"), lax.axis_index("tile")
    x, y, z = group // 8, (group // 2) % 4, (group % 2) * 8 + tile // 2
    high_z, core = group % 2, tile % 2
    def copy(src, dst, sends, recvs, target):
        pltpu.make_async_remote_copy(
            src_ref=src, dst_ref=dst, send_sem=sends, recv_sem=recvs, device_id=target, device_id_type=MESH
        ).start()

    def arrived(like, sem):
        pltpu.make_async_copy(like, like, sem).wait()

    def along(axis, d):
        if axis == 0:
            return device((x + d) % 4, y, z, core)
        return device(x, (y + d) % 4, z, core)

    beyond = device(x, y, (z + 15 + 2 * core) % 16, 1 - core)
    partner = device(x, y, z, 1 - core)
    below = {"grp": (x * 4 + y) * 2 + ((z * 2 + core + 31) % 32) // 16, "tile": (tile + 15) % 16}
    above = {"grp": (x * 4 + y) * 2 + ((z * 2 + core + 1) % 32) // 16, "tile": (tile + 1) % 16}

    planes = 8 // CHUNKS
    chunk = [pl.ds(k * planes, planes) for k in range(CHUNKS)]
    chunks = range(CHUNKS)
    loads = [pltpu.make_async_copy(noise_in, noise, local_sem.at[0]), pltpu.make_async_copy(source_in, source, local_sem.at[0])]
    for k in chunks:
        loads.append(pltpu.make_async_copy(potential.at[chunk[k]], pot_got[k].at[0], local_sem.at[1]))
        loads.append(pltpu.make_async_copy(log_cond.at[chunk[k]], cond_got[k].at[0], local_sem.at[2]))

    barrier = pltpu.get_barrier_semaphore()
    greeted = [device((x + a) % 4, (y + b) % 4, z, core) for a in range(4) for b in range(4) if a or b]
    greeted += [device(x, y, (z + d) % 16, core) for d in range(1, 16)]
    greeted += [beyond, partner]
    for other in greeted:
        pl.semaphore_signal(barrier, inc=1, device_id=other, device_id_type=MESH)
    for c in loads:
        c.start()
    pl.semaphore_wait(barrier, len(greeted))

    across = device(x, y, (z + 8) % 16, core)
    for k in chunks:
        copy(log_cond.at[chunk[k]], cond_got[k].at[4], send_sem.at[2], recv_z.at[0, k], across)

    def gather(src, got, first, k, kind):
        for d in range(1, 4):
            copy(src, got.at[first + d], send_sem.at[0], recv_gather.at[kind, k], along(0, d))

    for k in chunks:
        gather(potential.at[chunk[k]], pot_got[k], 0, k, 0)

    for ref, start, width in ((noise_in.at[0], 0, 4), (noise_in.at[1], 4, 2), (source_in, 6, 3)):
        copy(ref.at[pl.ds(0, width)], halo.at[1, pl.ds(start, width)], send_sem.at[3], recv_sem.at[0], below)
        copy(ref.at[pl.ds(8 - width, width)], halo.at[0, pl.ds(start, width)], send_sem.at[3], recv_sem.at[0], above)
    for k in chunks:
        gather(log_cond.at[chunk[k]], cond_got[k], 0, k, 1)

    wbuf[0, 0] = jnp.full((8, 128), weights[0], F32)
    for d in range(1, 4):
        copy(wbuf.at[0, 0], wbuf.at[0, d], send_sem.at[5], recv_sem.at[2], along(0, d))

    def parent(a, b, c):
        return parents[(a * 4 + b) * 2 + c]

    def spread(k, kind):
        to_z = 1 - high_z if kind == 1 else high_z
        for d in (2, 1, 3, 0):
            p = parent(x, (y + d) % 4, to_z)
            slot = (x - p // 8 + 4) % 4
            if kind == 2:
                block = cond_got[k][((p + high_z) % 2) * 4 + slot]
            else:
                block = pot_got[k][slot]
            if d == 0:
                picked[kind][k][0] = block
            else:
                sent[kind, k, d - 1] = block
                copy(sent.at[kind, k, d - 1], picked[kind][k].at[d], send_sem.at[1], recv_pick.at[kind, k], along(1, d))

    def choose(k, kind):
        arrived(picked[kind][k].at[pl.ds(1, 3)], recv_pick.at[kind, k])
        p = parent(x, y, 1 - high_z if kind == 1 else high_z)
        return picked[kind][k][(y - (p // 2) % 4 + 4) % 4]

    arrived(sent.at[0], local_sem.at[0])
    arrived(noise.at[0], local_sem.at[1])
    arrived(noise.at[0], local_sem.at[2])
    for k in chunks:
        arrived(pot_got[k].at[pl.ds(1, 3)], recv_gather.at[0, k])
        spread(k, 1)
    for k in chunks:
        zsent[k] = choose(k, 1)
        copy(zsent.at[k], zgot.at[k], send_sem.at[2], recv_z.at[1, k], across)
    for k in chunks:
        spread(k, 0)
    for k in chunks:
        arrived(cond_got[k].at[4], recv_z.at[0, k])
        gather(cond_got[k].at[4], cond_got[k], 4, k, 2)

    arrived(wbuf.at[0, pl.ds(1, 3)], recv_sem.at[2])
    wbuf[1, 0] = wbuf[0, 0] + wbuf[0, 1] + wbuf[0, 2] + wbuf[0, 3]
    for d in range(1, 4):
        copy(wbuf.at[1, 0], wbuf.at[1, d], send_sem.at[6], recv_sem.at[3], along(1, d))

    for k in chunks:
        arrived(cond_got[k].at[pl.ds(1, 3)], recv_gather.at[1, k])
        arrived(cond_got[k].at[pl.ds(5, 3)], recv_gather.at[2, k])
        spread(k, 2)

    from_here = jnp.full((1, 32, 128), (parent(x, y, high_z) % 2 == high_z).astype(jnp.int32)) > 0
    interior = pl.ds(HALO, 8)

    def place(f, k, value):
        start = k * planes
        field[f, pl.ds(HALO + start, planes)] = value
        src = field.at[f, pl.ds(HALO + start, planes)]
        if start < HALO:
            copy(src, field.at[f, pl.ds(HALO + 8 + start, planes)], send_sem.at[4], recv_sem.at[1], below)
        else:
            copy(src, field.at[f, pl.ds(start - HALO, planes)], send_sem.at[4], recv_sem.at[1], above)

    for k in chunks:
        place(0, k, choose(k, 2))
    for k in chunks:
        own = choose(k, 0)
        arrived(zgot.at[k], recv_z.at[1, k])
        place(1, k, jnp.where(from_here, own, zgot[k]))

    arrived(wbuf.at[1, pl.ds(1, 3)], recv_sem.at[3])
    wbuf[2, 0] = wbuf[1, 0] + wbuf[1, 1] + wbuf[1, 2] + wbuf[1, 3]
    copy(wbuf.at[2, 0], wbuf.at[2, 1], send_sem.at[7], recv_sem.at[4], across)

    arrived(halo, recv_sem.at[0])
    arrived(field.at[0], recv_sem.at[1])

    has_below = jnp.full((32, 128), (tile > 0).astype(jnp.int32))
    has_above = jnp.full((32, 128), (tile < 15).astype(jnp.int32))

    def inside(i, value):
        if i < HALO:
            return jnp.where(has_below > 0, value, 0.0)
        if i >= HALO + 8:
            return jnp.where(has_above > 0, value, 0.0)
        return value

    for f in range(2):
        for i in (*range(HALO), *range(HALO + 8, 2 * HALO + 8)):
            field[f, i] = inside(i, field[f, i])

    def border(ref, start, width, i):
        if i < HALO:
            return halo[0, start + width - HALO + i]
        if i >= HALO + 8:
            return halo[1, start + i - HALO - 8]
        return ref[i - HALO]

    def sweep(i, v_at):
        here, low, up = v_at(i), v_at(i - 1), v_at(i + 1)
        k = kcon[i]
        kv = k * here
        near = low + up + shifted(here, 0, 0.0) + shifted(here, 1, 0.0)
        weighted = kcon[i - 1] * low + kcon[i + 1] * up + shifted(kv, 0, 0.0) + shifted(kv, 1, 0.0)
        return k, near, weighted, here

    for m in range(2):
        edge = 2 * m
        last = 2 * HALO + 8 - edge
        for i in range(edge, last):
            fresh = border(noise.at[m], 0 if m == 0 else 4, 4 if m == 0 else 2, i)
            value = inside(i, 0.8 * field[0, i] + 0.6 * fresh)
            prop[i] = value
            kcon[i] = jnp.exp(value)
        flag = jnp.full((32, 128), accept[m]) > 0
        for i in range(edge + 1, last - 1):
            k, near, weighted, here = sweep(i, lambda j: field[1, j])
            inv[i] = 0.8 / (6.0 * k + kcon[i - 1] + kcon[i + 1] + shifted(k, 0, 1.0) + shifted(k, 1, 1.0))
            value = 0.2 * here + (2.0 * border(source, 6, 3, i) + k * near + weighted) * inv[i]
            once[i] = inside(i, value)
        if m == 0:
            arrived(field.at[0], send_sem.at[4])
        for i in range(edge + 2, last - 2):
            k, near, weighted, here = sweep(i, lambda j: once[j])
            value = 0.2 * here + (2.0 * border(source, 6, 3, i) + k * near + weighted) * inv[i]
            field[0, i] = jnp.where(flag, prop[i], field[0, i])
            field[1, i] = jnp.where(flag, inside(i, value), field[1, i])

    final = field[1, interior]
    cond_out[...] = field[0, interior]
    pot_out[...] = final

    for d in range(1, 4):
        at = pl.ds(HALO + 2 * ((y + d) % 4), 2)
        copy(field.at[1, at], cols.at[0, d], send_sem.at[8], recv_rows.at[0, d], along(1, d))
    cols[0, 0] = field[1, pl.ds(HALO + 2 * y, 2)]
    scaled = final * weights[0]
    into = lax.broadcasted_iota(jnp.int32, (512, 512), 0)
    out = lax.broadcasted_iota(jnp.int32, (512, 512), 1)
    wanted = ((out // 16) % 4) * 128 + ((out // 64) % 2) * 64 + (out // 128) * 16 + out % 16
    select = jnp.where(into == wanted, 1.0, 0.0).astype(BF16)
    stacked = jnp.concatenate(
        [jnp.concatenate([scaled[4 * half + j] for j in range(4)], axis=1) for half in range(2)], axis=0
    )
    high, low = split(stacked)
    shuffled = jnp.dot(high, select, preferred_element_type=F32) + jnp.dot(low, select, preferred_element_type=F32)
    for j in range(4):
        for half in range(2):
            perm[j, half] = shuffled[32 * half : 32 * half + 32, 128 * j : 128 * j + 128]
    for d in range(1, 4):
        copy(perm.at[(x + d) % 4], rows.at[0, d], send_sem.at[9], recv_rows.at[1, d], along(0, d))
    rows[0, 0] = perm[x]

    def forward(src, axis, n):
        for d in range(1, 4):
            copy(src.at[0, n], src.at[d, n], send_sem.at[10 + axis], recv_rows.at[axis, 0], along(axis, d))

    forward(cols, 0, 0)
    forward(rows, 1, 0)
    for n in range(1, 4):
        arrived(cols.at[0, n], recv_rows.at[0, n])
        forward(cols, 0, n)
        arrived(rows.at[0, n], recv_rows.at[1, n])
        forward(rows, 1, n)
    arrived(cols.at[pl.ds(1, 3)], recv_rows.at[0, 0])
    arrived(rows.at[pl.ds(1, 3)], recv_rows.at[1, 0])

    right = jnp.concatenate(
        [jnp.concatenate([cols[dx, dy, 0], cols[dx, dy, 1]], axis=1) for dy in range(4) for dx in range(4)], axis=0
    )
    right_high, right_low = split(right)
    for half in range(2):
        left = jnp.concatenate([rows[dy, dx, half] for dy in range(4) for dx in range(4)], axis=0).T
        left_high, left_low = split(left)
        product = (
            jnp.dot(left_high, right_high, preferred_element_type=F32)
            + jnp.dot(left_high, right_low, preferred_element_type=F32)
            + jnp.dot(left_low, right_high, preferred_element_type=F32)
        )
        for c in range(2):
            partial[c, half] = product[64 * c : 64 * c + 64]
    copy(partial.at[1 - core], corner, send_sem.at[12], recv_sem.at[5], partner)
    arrived(corner, recv_sem.at[5])
    for half in range(2):
        total = partial[core, half] + corner[half]
        for j in range(4):
            summed[4 * half + j] = total[16 * j : 16 * j + 16]
    for d in sorted(range(1, 16), key=lambda d: -min(d, 16 - d)):
        copy(summed.at[(z + d) % 8], zsum.at[d], send_sem.at[13], recv_sem.at[6], device(x, y, (z + d) % 16, core))
    arrived(wbuf.at[2, 1], recv_sem.at[4])
    arrived(zsum.at[pl.ds(1, 15)], recv_sem.at[6])
    total = summed[z % 8]
    for d in range(1, 16):
        total = total + zsum[d]
    weight_sum = wbuf[2, 0] + wbuf[2, 1]
    piece = mom_out.at[pl.ds(pl.multiple_of(x * 16, 16), 16), pl.ds(pl.multiple_of(y * 256, 256), 256)]
    piece[...] = total / weight_sum[0:1, 0:1]
    for a in range(4):
        for b in range(4):
            if a or b:
                copy(piece, piece, send_sem.at[14], recv_sem.at[7], device((x + a) % 4, (y + b) % 4, z, core))
    arrived(zsum.at[pl.ds(1, 15)], recv_sem.at[7])
    many = zsum.at[pl.ds(1, 15)]
    three = rows.at[0, pl.ds(1, 3)]
    most = rows.at[pl.ds(1, 3)]
    works = wbuf.at[0, pl.ds(1, 3)]
    likes = (sent, sent, field.at[0], halo, None, works, works, wbuf.at[2, 1], three, three, most, most, corner, many, many)
    for i, like in enumerate(likes):
        if like is not None:
            arrived(like, send_sem.at[i])


def local(log_cond, potential, noise, source, parents, accept, weights):
    hbm = pl.BlockSpec(memory_space=pl.ANY)
    vmem, smem = pl.BlockSpec(memory_space=pltpu.VMEM), pl.BlockSpec(memory_space=pltpu.SMEM)
    dma = pltpu.SemaphoreType.DMA
    block = (8, 32, 128)
    part = (8 // CHUNKS, 32, 128)
    wide = (2 * HALO + 8, 32, 128)
    conduct, pot, moments = pl.pallas_call(
        kernel,
        out_shape=(
            pltpu.VMEM(block, F32),
            pltpu.VMEM(block, F32),
            pltpu.VMEM((64, 1024), F32),
        ),
        in_specs=[hbm, hbm, hbm, hbm, smem, smem, smem],
        out_specs=(vmem, vmem, vmem),
        scratch_shapes=[
            (pltpu.VMEM((4, *part), F32),) * CHUNKS,
            (pltpu.VMEM((8, *part), F32),) * CHUNKS,
            pltpu.VMEM((3, CHUNKS, 3, *part), F32),
            ((pltpu.VMEM((4, *part), F32),) * CHUNKS,) * 3,
            pltpu.VMEM((CHUNKS, *part), F32),
            pltpu.VMEM((CHUNKS, *part), F32),
            pltpu.VMEM((2, 9, 32, 128), F32),
            pltpu.VMEM((2, *wide), F32),
            pltpu.VMEM(wide, F32),
            pltpu.VMEM(wide, F32),
            pltpu.VMEM(wide, F32),
            pltpu.VMEM(wide, F32),
            pltpu.VMEM((2, *block), F32),
            pltpu.VMEM(block, F32),
            pltpu.VMEM((4, 2, 32, 128), F32),
            pltpu.VMEM((4, 4, 2, 32, 128), F32),
            pltpu.VMEM((4, 4, 2, 32, 128), F32),
            pltpu.VMEM((2, 2, 64, 256), F32),
            pltpu.VMEM((2, 64, 256), F32),
            pltpu.VMEM((8, 16, 256), F32),
            pltpu.VMEM((16, 16, 256), F32),
            pltpu.VMEM((3, 4, 8, 128), F32),
            dma((15,)), dma((3, CHUNKS)), dma((3, CHUNKS)), dma((2, CHUNKS)), dma((2, 4)), dma((8,)), dma((3,)),
        ],
        compiler_params=pltpu.CompilerParams(collective_id=0, has_side_effects=True),
        name="resample_move",
    )(log_cond[0], potential[0], noise[:, 0], source, parents, accept.reshape(-1), weights)
    return conduct[None], pot[None], moments


def solution(mesh):
    placed = (
        P("grp", "tile", None, None),
        P("grp", "tile", None, None),
        P(None, "grp", "tile", None, None),
        P("tile", None, None),
        P(),
        P(None, "grp"),
        P("grp"),
    )
    return jax.shard_map(
        local,
        mesh=mesh,
        in_specs=placed,
        out_specs=(P("grp", "tile", None, None), P("grp", "tile", None, None), P("tile", None)),
        check_vma=False,
    )
```

time: 91.9 us -> 86.2 us (0.938)
  Pallas kernels: 87.5 us -> 82.8 us
  local copies, waits for them, and re-layouts: 2.98 us -> 2.01 us
    pallas_call x1, Pallas kernels: 87.5 us -> 82.8 us  [local(): pl.pallas_call(kernel, out_shape=(pltpu.VMEM(block, F32), pltpu.VMEM(bloc...]
    unnamed x7 -> x3, local copies, waits for them, and re-layouts: 2.98 us -> 2.01 us
where the time goes in v3:
time: 86.2 us; the launch traced here: 86.1 us
  Pallas kernels  82.8 us (96%)
  local copies, waits for them, and re-layouts  2.01 us (2%)
  between operations  1.29 us (1%)
    pallas_call x1, Pallas kernels, local(): pl.pallas_call(kernel, out_shape=(pltpu.VMEM(block, F32), pltpu.VMEM(bloc...  82.8 us
    unnamed x3, local copies, waits for them, and re-layouts  2.01 us

profile of v3, /device:TPU:1, one launch (start us, length us, event | category | flops | bytes accessed | tf_op | source)
XLA Modules:
  0.0 86.1 jit_solution(13757004163507693253)
XLA Ops:
  1.3 82.8 %resample_move.1 = (f32[8,32,128]{2,1,0:T(8,128)S(1)}, f32[8,32,128]{2,1,0:T(8,128)S(1)}, f32[64,1024]{1,0:T(8,128)S(1)}) custom-call(f32[8,32,128]{2,1,0:T(8,128)} %bitcast.9, f32[8,32,128]{2,1,0:T(8,128)} %bitcast.10, f32[2,8,32,128]{3,2,1,0:T(8,128)} %bitcast.8, f32[8,32,128]{2,1,0:T(8,128)} %source_in.1, s32[32]{0:T(128)} %parents.1, s32[2]{0:T(128)} %bitcast.11, ...), custom_call_target="tpu_custom_call" | custom-call | tf_op jit(solution)/shard_map/resample_move/pallas_call | solution.py:315
  84.1 0.7 copy.13
  84.7 0.7 copy.14
  85.4 0.7 copy.15

commit v4 on v3

--- a/solution.py
+++ b/solution.py
@@ -30,10 +30,10 @@
 
 
 def kernel(
-    log_cond, potential, noise_in, source_in, parents, accept, weights,
+    log_cond, potential, noise_in, source_in, parents_in, accept_in, weights_in,
     cond_out, pot_out, mom_out,
     pot_got, cond_got, sent, picked, zsent, zgot, halo, field, prop, kcon, inv, once,
-    noise, source, perm, rows, cols, partial, corner, summed, zsum, wbuf,
+    parents, accept, weights, noise, source, perm, rows, cols, partial, corner, summed, zsum, wbuf,
     send_sem, recv_gather, recv_pick, recv_z, recv_rows, recv_sem, local_sem,
 ):
     group, tile = lax.axis_index("grp"), lax.axis_index("tile")
@@ -52,8 +52,6 @@
             return device((x + d) % 4, y, z, core)
         return device(x, (y + d) % 4, z, core)
 
-    beyond = device(x, y, (z + 15 + 2 * core) % 16, 1 - core)
-    partner = device(x, y, z, 1 - core)
     below = {"grp": (x * 4 + y) * 2 + ((z * 2 + core + 31) % 32) // 16, "tile": (tile + 15) % 16}
     above = {"grp": (x * 4 + y) * 2 + ((z * 2 + core + 1) % 32) // 16, "tile": (tile + 1) % 16}
 
@@ -61,17 +59,21 @@
     chunk = [pl.ds(k * planes, planes) for k in range(CHUNKS)]
     chunks = range(CHUNKS)
     loads = [pltpu.make_async_copy(noise_in, noise, local_sem.at[0]), pltpu.make_async_copy(source_in, source, local_sem.at[0])]
+    scalars = [
+        pltpu.make_async_copy(src, dst, local_sem.at[3 + i])
+        for i, (src, dst) in enumerate(((parents_in, parents), (accept_in, accept), (weights_in, weights)))
+    ]
     for k in chunks:
         loads.append(pltpu.make_async_copy(potential.at[chunk[k]], pot_got[k].at[0], local_sem.at[1]))
         loads.append(pltpu.make_async_copy(log_cond.at[chunk[k]], cond_got[k].at[0], local_sem.at[2]))
 
     barrier = pltpu.get_barrier_semaphore()
     greeted = [device((x + a) % 4, (y + b) % 4, z, core) for a in range(4) for b in range(4) if a or b]
-    greeted += [device(x, y, (z + d) % 16, core) for d in range(1, 16)]
-    greeted += [beyond, partner]
+    greeted += [device(x, y, (z + d) % 16, core) for d in (8, 6, 10, 4, 12, 2, 14, 1, 15)]
+    greeted += [device(x, y, (z + d) % 16, 1 - core) for d in (0, 1, 15)]
     for other in greeted:
         pl.semaphore_signal(barrier, inc=1, device_id=other, device_id_type=MESH)
-    for c in loads:
+    for c in scalars + loads:
         c.start()
     pl.semaphore_wait(barrier, len(greeted))
 
@@ -92,6 +94,8 @@
     for k in chunks:
         gather(log_cond.at[chunk[k]], cond_got[k], 0, k, 1)
 
+    for c in scalars:
+        c.wait()
     wbuf[0, 0] = jnp.full((8, 128), weights[0], F32)
     for d in range(1, 4):
         copy(wbuf.at[0, 0], wbuf.at[0, d], send_sem.at[5], recv_sem.at[2], along(0, d))
@@ -273,19 +277,21 @@
             + jnp.dot(left_low, right_high, preferred_element_type=F32)
         )
         for c in range(2):
-            partial[c, half] = product[64 * c : 64 * c + 64]
-    copy(partial.at[1 - core], corner, send_sem.at[12], recv_sem.at[5], partner)
+            for j in range(4):
+                partial[j % 2, c, 2 * half + j // 2] = product[64 * c + 16 * j : 64 * c + 16 * j + 16]
+    parity = z % 2
+    beside = z + 1 - 2 * parity
+    copy(partial.at[1 - parity, core], corner.at[1], send_sem.at[12], recv_sem.at[5], device(x, y, beside, core))
+    copy(partial.at[1 - parity, 1 - core], corner.at[2], send_sem.at[12], recv_sem.at[5], device(x, y, beside, 1 - core))
+    copy(partial.at[parity, 1 - core], corner.at[0], send_sem.at[12], recv_sem.at[5], device(x, y, z, 1 - core))
     arrived(corner, recv_sem.at[5])
-    for half in range(2):
-        total = partial[core, half] + corner[half]
-        for j in range(4):
-            summed[4 * half + j] = total[16 * j : 16 * j + 16]
-    for d in sorted(range(1, 16), key=lambda d: -min(d, 16 - d)):
-        copy(summed.at[(z + d) % 8], zsum.at[d], send_sem.at[13], recv_sem.at[6], device(x, y, (z + d) % 16, core))
+    summed[...] = (partial[parity, core] + corner[0]) + (corner[1] + corner[2])
+    for d in (8, 6, 10, 4, 12, 2, 14):
+        copy(summed.at[((z + d) % 8) // 2], zsum.at[d // 2], send_sem.at[13], recv_sem.at[6], device(x, y, (z + d) % 16, core))
     arrived(wbuf.at[2, 1], recv_sem.at[4])
-    arrived(zsum.at[pl.ds(1, 15)], recv_sem.at[6])
-    total = summed[z % 8]
-    for d in range(1, 16):
+    arrived(zsum.at[pl.ds(1, 7)], recv_sem.at[6])
+    total = summed[(z % 8) // 2]
+    for d in range(1, 8):
         total = total + zsum[d]
     weight_sum = wbuf[2, 0] + wbuf[2, 1]
     piece = mom_out.at[pl.ds(pl.multiple_of(x * 16, 16), 16), pl.ds(pl.multiple_of(y * 256, 256), 256)]
@@ -299,15 +305,26 @@
     three = rows.at[0, pl.ds(1, 3)]
     most = rows.at[pl.ds(1, 3)]
     works = wbuf.at[0, pl.ds(1, 3)]
-    likes = (sent, sent, field.at[0], halo, None, works, works, wbuf.at[2, 1], three, three, most, most, corner, many, many)
+    likes = (sent, sent, field.at[0], halo, None, works, works, wbuf.at[2, 1], three, three, most, most, corner, zsum.at[pl.ds(1, 7)], many)
     for i, like in enumerate(likes):
         if like is not None:
             arrived(like, send_sem.at[i])
 
 
+def leave(cond, pot, mom, cond_out, pot_out, mom_out, sems):
+    copies = [
+        pltpu.make_async_copy(src, dst, sems.at[i])
+        for i, (src, dst) in enumerate(((mom, mom_out), (cond, cond_out), (pot, pot_out)))
+    ]
+    for c in copies:
+        c.start()
+    for c in copies:
+        c.wait()
+
+
 def local(log_cond, potential, noise, source, parents, accept, weights):
     hbm = pl.BlockSpec(memory_space=pl.ANY)
-    vmem, smem = pl.BlockSpec(memory_space=pltpu.VMEM), pl.BlockSpec(memory_space=pltpu.SMEM)
+    vmem = pl.BlockSpec(memory_space=pltpu.VMEM)
     dma = pltpu.SemaphoreType.DMA
     block = (8, 32, 128)
     part = (8 // CHUNKS, 32, 128)
@@ -319,7 +336,7 @@
             pltpu.VMEM(block, F32),
             pltpu.VMEM((64, 1024), F32),
         ),
-        in_specs=[hbm, hbm, hbm, hbm, smem, smem, smem],
+        in_specs=[hbm] * 7,
         out_specs=(vmem, vmem, vmem),
         scratch_shapes=[
             (pltpu.VMEM((4, *part), F32),) * CHUNKS,
@@ -334,21 +351,36 @@
             pltpu.VMEM(wide, F32),
             pltpu.VMEM(wide, F32),
             pltpu.VMEM(wide, F32),
+            pltpu.SMEM((32,), jnp.int32),
+            pltpu.SMEM((2,), jnp.int32),
+            pltpu.SMEM((1,), F32),
             pltpu.VMEM((2, *block), F32),
             pltpu.VMEM(block, F32),
             pltpu.VMEM((4, 2, 32, 128), F32),
             pltpu.VMEM((4, 4, 2, 32, 128), F32),
             pltpu.VMEM((4, 4, 2, 32, 128), F32),
-            pltpu.VMEM((2, 2, 64, 256), F32),
-            pltpu.VMEM((2, 64, 256), F32),
-            pltpu.VMEM((8, 16, 256), F32),
+            pltpu.VMEM((2, 2, 4, 16, 256), F32),
+            pltpu.VMEM((3, 4, 16, 256), F32),
+            pltpu.VMEM((4, 16, 256), F32),
             pltpu.VMEM((16, 16, 256), F32),
             pltpu.VMEM((3, 4, 8, 128), F32),
-            dma((15,)), dma((3, CHUNKS)), dma((3, CHUNKS)), dma((2, CHUNKS)), dma((2, 4)), dma((8,)), dma((3,)),
+            dma((15,)), dma((3, CHUNKS)), dma((3, CHUNKS)), dma((2, CHUNKS)), dma((2, 4)), dma((8,)), dma((6,)),
         ],
         compiler_params=pltpu.CompilerParams(collective_id=0, has_side_effects=True),
         name="resample_move",
     )(log_cond[0], potential[0], noise[:, 0], source, parents, accept.reshape(-1), weights)
+    conduct, pot, moments = pl.pallas_call(
+        leave,
+        out_shape=(
+            jax.ShapeDtypeStruct(block, F32),
+            jax.ShapeDtypeStruct(block, F32),
+            jax.ShapeDtypeStruct((64, 1024), F32),
+        ),
+        in_specs=[hbm] * 3,
+        out_specs=(hbm, hbm, hbm),
+        scratch_shapes=[dma((3,))],
+        name="leave",
+    )(*(pltpu.with_memory_space_constraint(value, pltpu.VMEM) for value in (conduct, pot, moments)))
     return conduct[None], pot[None], moments
 
 

time: 86.2 us -> 84.2 us (0.977)
  local copies, waits for them, and re-layouts: 2.01 us -> 0 us
    unnamed x3 -> x0, local copies, waits for them, and re-layouts: 2.01 us -> none
where the time goes in v4:
time: 84.2 us; the launch traced here: 84 us
  Pallas kernels  82.8 us (98%)
  between operations  1.29 us (2%)
    pallas_call x1, Pallas kernels, local(): pl.pallas_call(kernel, out_shape=(pltpu.VMEM(block, F32), pltpu.VMEM(bloc...  81.9 us

profile of v4, /device:TPU:1, one launch (start us, length us, event | category | flops | bytes accessed | tf_op | source)
XLA Modules:
  0.0 84.0 jit_solution(9221163506924453716)
XLA Ops:
  1.3 81.9 %resample_move.1 = (f32[8,32,128]{2,1,0:T(8,128)S(1)}, f32[8,32,128]{2,1,0:T(8,128)S(1)}, f32[64,1024]{1,0:T(8,128)S(1)}) custom-call(f32[8,32,128]{2,1,0:T(8,128)} %bitcast.7, f32[8,32,128]{2,1,0:T(8,128)} %bitcast.8, f32[2,8,32,128]{3,2,1,0:T(8,128)} %bitcast.6, f32[8,32,128]{2,1,0:T(8,128)} %source_in.1, s32[32]{0:T(128)} %parents_in.1, s32[2]{0:T(128)} %bitcast.9, ...), custom_call_target="tpu_custom_call" | custom-call | tf_op jit(solution)/shard_map/resample_move/pallas_call | solution.py:332
  83.2 0.8 leave.1

commit v5 on v4

--- a/solution.py
+++ b/solution.py
@@ -10,6 +10,7 @@
 BF16 = jnp.bfloat16
 CHUNKS = 4
 HALO = 4
+FAR_FIRST = (2, 1, 3)
 
 
 def device(x, y, z, core):
@@ -33,8 +34,8 @@
     log_cond, potential, noise_in, source_in, parents_in, accept_in, weights_in,
     cond_out, pot_out, mom_out,
     pot_got, cond_got, sent, picked, zsent, zgot, halo, field, prop, kcon, inv, once,
-    parents, accept, weights, noise, source, perm, rows, cols, partial, corner, summed, zsum, wbuf,
-    send_sem, recv_gather, recv_pick, recv_z, recv_rows, recv_sem, local_sem,
+    parents, accept, weights, noise, source, select, perm, rows, cols, partial, corner, summed, zsum, wbuf,
+    send_sem, recv_gather, recv_pick, recv_z, recv_rows, recv_pair, recv_sem, local_sem,
 ):
     group, tile = lax.axis_index("grp"), lax.axis_index("tile")
     x, y, z = group // 8, (group // 2) % 4, (group % 2) * 8 + tile // 2
@@ -82,7 +83,7 @@
         copy(log_cond.at[chunk[k]], cond_got[k].at[4], send_sem.at[2], recv_z.at[0, k], across)
 
     def gather(src, got, first, k, kind):
-        for d in range(1, 4):
+        for d in FAR_FIRST:
             copy(src, got.at[first + d], send_sem.at[0], recv_gather.at[kind, k], along(0, d))
 
     for k in chunks:
@@ -105,7 +106,7 @@
 
     def spread(k, kind):
         to_z = 1 - high_z if kind == 1 else high_z
-        for d in (2, 1, 3, 0):
+        for d in (*FAR_FIRST, 0):
             p = parent(x, (y + d) % 4, to_z)
             slot = (x - p // 8 + 4) % 4
             if kind == 2:
@@ -126,17 +127,32 @@
     arrived(sent.at[0], local_sem.at[0])
     arrived(noise.at[0], local_sem.at[1])
     arrived(noise.at[0], local_sem.at[2])
-    for k in chunks:
+    def cross(k):
         arrived(pot_got[k].at[pl.ds(1, 3)], recv_gather.at[0, k])
         spread(k, 1)
-    for k in chunks:
+
+    def leave_side(k):
         zsent[k] = choose(k, 1)
         copy(zsent.at[k], zgot.at[k], send_sem.at[2], recv_z.at[1, k], across)
-    for k in chunks:
-        spread(k, 0)
-    for k in chunks:
+
+    def pass_on(k):
         arrived(cond_got[k].at[4], recv_z.at[0, k])
         gather(cond_got[k].at[4], cond_got[k], 4, k, 2)
+
+    cross(0)
+    cross(1)
+    leave_side(0)
+    cross(2)
+    leave_side(1)
+    cross(3)
+    pass_on(0)
+    leave_side(2)
+    pass_on(1)
+    leave_side(3)
+    for k in chunks:
+        spread(k, 0)
+    pass_on(2)
+    pass_on(3)
 
     arrived(wbuf.at[0, pl.ds(1, 3)], recv_sem.at[2])
     wbuf[1, 0] = wbuf[0, 0] + wbuf[0, 1] + wbuf[0, 2] + wbuf[0, 3]
@@ -171,6 +187,10 @@
     wbuf[2, 0] = wbuf[1, 0] + wbuf[1, 1] + wbuf[1, 2] + wbuf[1, 3]
     copy(wbuf.at[2, 0], wbuf.at[2, 1], send_sem.at[7], recv_sem.at[4], across)
 
+    into = lax.broadcasted_iota(jnp.int32, (512, 512), 0)
+    out = lax.broadcasted_iota(jnp.int32, (512, 512), 1)
+    wanted = ((out // 16) % 4) * 128 + ((out // 64) % 2) * 64 + (out // 128) * 16 + out % 16
+    select[...] = jnp.where(into == wanted, 1.0, 0.0).astype(BF16)
     arrived(halo, recv_sem.at[0])
     arrived(field.at[0], recv_sem.at[1])
 
@@ -229,34 +249,30 @@
     cond_out[...] = field[0, interior]
     pot_out[...] = final
 
-    for d in range(1, 4):
+    for d in FAR_FIRST:
         at = pl.ds(HALO + 2 * ((y + d) % 4), 2)
         copy(field.at[1, at], cols.at[0, d], send_sem.at[8], recv_rows.at[0, d], along(1, d))
     cols[0, 0] = field[1, pl.ds(HALO + 2 * y, 2)]
     scaled = final * weights[0]
-    into = lax.broadcasted_iota(jnp.int32, (512, 512), 0)
-    out = lax.broadcasted_iota(jnp.int32, (512, 512), 1)
-    wanted = ((out // 16) % 4) * 128 + ((out // 64) % 2) * 64 + (out // 128) * 16 + out % 16
-    select = jnp.where(into == wanted, 1.0, 0.0).astype(BF16)
     stacked = jnp.concatenate(
         [jnp.concatenate([scaled[4 * half + j] for j in range(4)], axis=1) for half in range(2)], axis=0
     )
     high, low = split(stacked)
-    shuffled = jnp.dot(high, select, preferred_element_type=F32) + jnp.dot(low, select, preferred_element_type=F32)
+    shuffled = jnp.dot(high, select[...], preferred_element_type=F32) + jnp.dot(low, select[...], preferred_element_type=F32)
     for j in range(4):
         for half in range(2):
             perm[j, half] = shuffled[32 * half : 32 * half + 32, 128 * j : 128 * j + 128]
-    for d in range(1, 4):
+    for d in FAR_FIRST:
         copy(perm.at[(x + d) % 4], rows.at[0, d], send_sem.at[9], recv_rows.at[1, d], along(0, d))
     rows[0, 0] = perm[x]
 
     def forward(src, axis, n):
-        for d in range(1, 4):
+        for d in FAR_FIRST:
             copy(src.at[0, n], src.at[d, n], send_sem.at[10 + axis], recv_rows.at[axis, 0], along(axis, d))
 
     forward(cols, 0, 0)
     forward(rows, 1, 0)
-    for n in range(1, 4):
+    for n in (1, 3, 2):
         arrived(cols.at[0, n], recv_rows.at[0, n])
         forward(cols, 0, n)
         arrived(rows.at[0, n], recv_rows.at[1, n])
@@ -268,44 +284,51 @@
         [jnp.concatenate([cols[dx, dy, 0], cols[dx, dy, 1]], axis=1) for dy in range(4) for dx in range(4)], axis=0
     )
     right_high, right_low = split(right)
-    for half in range(2):
-        left = jnp.concatenate([rows[dy, dx, half] for dy in range(4) for dx in range(4)], axis=0).T
-        left_high, left_low = split(left)
-        product = (
-            jnp.dot(left_high, right_high, preferred_element_type=F32)
-            + jnp.dot(left_high, right_low, preferred_element_type=F32)
-            + jnp.dot(left_low, right_high, preferred_element_type=F32)
-        )
-        for c in range(2):
-            for j in range(4):
-                partial[j % 2, c, 2 * half + j // 2] = product[64 * c + 16 * j : 64 * c + 16 * j + 16]
+    lefts = [split(jnp.concatenate([rows[dy, dx, half] for dy in range(4) for dx in range(4)], axis=0).T) for half in range(2)]
+
     parity = z % 2
     beside = z + 1 - 2 * parity
-    copy(partial.at[1 - parity, core], corner.at[1], send_sem.at[12], recv_sem.at[5], device(x, y, beside, core))
-    copy(partial.at[1 - parity, 1 - core], corner.at[2], send_sem.at[12], recv_sem.at[5], device(x, y, beside, 1 - core))
-    copy(partial.at[parity, 1 - core], corner.at[0], send_sem.at[12], recv_sem.at[5], device(x, y, z, 1 - core))
-    arrived(corner, recv_sem.at[5])
-    summed[...] = (partial[parity, core] + corner[0]) + (corner[1] + corner[2])
-    for d in (8, 6, 10, 4, 12, 2, 14):
-        copy(summed.at[((z + d) % 8) // 2], zsum.at[d // 2], send_sem.at[13], recv_sem.at[6], device(x, y, (z + d) % 16, core))
+    for h in range(2):
+        lanes = slice(128 * h, 128 * h + 128)
+        for half in range(2):
+            left_high, left_low = lefts[half]
+            product = (
+                jnp.dot(left_high, right_high[:, lanes], preferred_element_type=F32)
+                + jnp.dot(left_high, right_low[:, lanes], preferred_element_type=F32)
+                + jnp.dot(left_low, right_high[:, lanes], preferred_element_type=F32)
+            )
+            for c in range(2):
+                for j in range(4):
+                    partial[h, j % 2, c, 2 * half + j // 2] = product[64 * c + 16 * j : 64 * c + 16 * j + 16]
+        for i, (across_z, other) in enumerate(((False, True), (True, False), (True, True))):
+            src = partial.at[h, 1 - parity if across_z else parity, 1 - core if other else core]
+            target = device(x, y, beside if across_z else z, 1 - core if other else core)
+            copy(src, corner.at[h, i], send_sem.at[12], recv_pair.at[0, h], target)
+    for h in range(2):
+        arrived(corner.at[h], recv_pair.at[0, h])
+        summed[h] = (partial[h, parity, core] + corner[h, 0]) + (corner[h, 1] + corner[h, 2])
+        for d in (8, 6, 10, 4, 12, 2, 14):
+            target = device(x, y, (z + d) % 16, core)
+            copy(summed.at[h, ((z + d) % 8) // 2], zsum.at[h, d // 2], send_sem.at[13], recv_pair.at[1, h], target)
     arrived(wbuf.at[2, 1], recv_sem.at[4])
-    arrived(zsum.at[pl.ds(1, 7)], recv_sem.at[6])
-    total = summed[(z % 8) // 2]
-    for d in range(1, 8):
-        total = total + zsum[d]
-    weight_sum = wbuf[2, 0] + wbuf[2, 1]
-    piece = mom_out.at[pl.ds(pl.multiple_of(x * 16, 16), 16), pl.ds(pl.multiple_of(y * 256, 256), 256)]
-    piece[...] = total / weight_sum[0:1, 0:1]
-    for a in range(4):
-        for b in range(4):
-            if a or b:
-                copy(piece, piece, send_sem.at[14], recv_sem.at[7], device((x + a) % 4, (y + b) % 4, z, core))
-    arrived(zsum.at[pl.ds(1, 15)], recv_sem.at[7])
-    many = zsum.at[pl.ds(1, 15)]
+    weight_sum = (wbuf[2, 0] + wbuf[2, 1])[0:1, 0:1]
+    for h in range(2):
+        arrived(zsum.at[h, pl.ds(1, 7)], recv_pair.at[1, h])
+        total = summed[h, (z % 8) // 2]
+        for d in range(1, 8):
+            total = total + zsum[h, d]
+        piece = mom_out.at[pl.ds(pl.multiple_of(x * 16, 16), 16), pl.ds(pl.multiple_of(y * 256 + 128 * h, 128), 128)]
+        piece[...] = total / weight_sum
+        for a in (2, 1, 3, 0):
+            for b in (2, 1, 3, 0):
+                if a or b:
+                    copy(piece, piece, send_sem.at[14], recv_sem.at[7], device((x + a) % 4, (y + b) % 4, z, core))
+    many = zsum.at[pl.ds(0, 2), pl.ds(1, 15)]
+    arrived(many, recv_sem.at[7])
     three = rows.at[0, pl.ds(1, 3)]
     most = rows.at[pl.ds(1, 3)]
     works = wbuf.at[0, pl.ds(1, 3)]
-    likes = (sent, sent, field.at[0], halo, None, works, works, wbuf.at[2, 1], three, three, most, most, corner, zsum.at[pl.ds(1, 7)], many)
+    likes = (sent, sent, field.at[0], halo, None, works, works, wbuf.at[2, 1], three, three, most, most, corner, zsum.at[pl.ds(0, 2), pl.ds(1, 7)], many)
     for i, like in enumerate(likes):
         if like is not None:
             arrived(like, send_sem.at[i])
@@ -336,7 +359,7 @@
             pltpu.VMEM(block, F32),
             pltpu.VMEM((64, 1024), F32),
         ),
-        in_specs=[hbm] * 7,
+        in_specs=[hbm] * 4 + [pl.BlockSpec(memory_space=pltpu.HBM)] * 3,
         out_specs=(vmem, vmem, vmem),
         scratch_shapes=[
             (pltpu.VMEM((4, *part), F32),) * CHUNKS,
@@ -356,15 +379,16 @@
             pltpu.SMEM((1,), F32),
             pltpu.VMEM((2, *block), F32),
             pltpu.VMEM(block, F32),
+            pltpu.VMEM((512, 512), BF16),
             pltpu.VMEM((4, 2, 32, 128), F32),
             pltpu.VMEM((4, 4, 2, 32, 128), F32),
             pltpu.VMEM((4, 4, 2, 32, 128), F32),
-            pltpu.VMEM((2, 2, 4, 16, 256), F32),
-            pltpu.VMEM((3, 4, 16, 256), F32),
-            pltpu.VMEM((4, 16, 256), F32),
-            pltpu.VMEM((16, 16, 256), F32),
+            pltpu.VMEM((2, 2, 2, 4, 16, 128), F32),
+            pltpu.VMEM((2, 3, 4, 16, 128), F32),
+            pltpu.VMEM((2, 4, 16, 128), F32),
+            pltpu.VMEM((2, 16, 16, 128), F32),
             pltpu.VMEM((3, 4, 8, 128), F32),
-            dma((15,)), dma((3, CHUNKS)), dma((3, CHUNKS)), dma((2, CHUNKS)), dma((2, 4)), dma((8,)), dma((6,)),
+            dma((15,)), dma((3, CHUNKS)), dma((3, CHUNKS)), dma((2, CHUNKS)), dma((2, 4)), dma((2, 2)), dma((8,)), dma((6,)),
         ],
         compiler_params=pltpu.CompilerParams(collective_id=0, has_side_effects=True),
         name="resample_move",

time: 84.2 us -> 83.3 us (0.989)
  Pallas kernels: 82.8 us -> 81.9 us
    pallas_call x1, Pallas kernels: 81.9 us -> 81.1 us  [local(): pl.pallas_call(kernel, out_shape=(pltpu.VMEM(block, F32), pltpu.VMEM(bloc...]
where the time goes in v5:
time: 83.3 us; the launch traced here: 83.2 us
  Pallas kernels  81.9 us (98%)
  between operations  1.29 us (2%)
    pallas_call x1, Pallas kernels, local(): pl.pallas_call(kernel, out_shape=(pltpu.VMEM(block, F32), pltpu.VMEM(bloc...  81.1 us

profile of v5, /device:TPU:1, one launch (start us, length us, event | category | flops | bytes accessed | tf_op | source)
XLA Modules:
  0.0 83.2 jit_solution(3833392599528878651)
XLA Ops:
  1.3 81.1 %resample_move.1 = (f32[8,32,128]{2,1,0:T(8,128)S(1)}, f32[8,32,128]{2,1,0:T(8,128)S(1)}, f32[64,1024]{1,0:T(8,128)S(1)}) custom-call(f32[8,32,128]{2,1,0:T(8,128)} %bitcast.7, f32[8,32,128]{2,1,0:T(8,128)} %bitcast.8, f32[2,8,32,128]{3,2,1,0:T(8,128)} %bitcast.6, f32[8,32,128]{2,1,0:T(8,128)} %source_in.1, s32[32]{0:T(128)} %parents_in.1, s32[2]{0:T(128)} %bitcast.9, ...), custom_call_target="tpu_custom_call" | custom-call | tf_op jit(solution)/shard_map/resample_move/pallas_call | solution.py:355
  82.4 0.8 leave.1

commit v6 on v5

--- a/solution.py
+++ b/solution.py
@@ -34,7 +34,7 @@
     log_cond, potential, noise_in, source_in, parents_in, accept_in, weights_in,
     cond_out, pot_out, mom_out,
     pot_got, cond_got, sent, picked, zsent, zgot, halo, field, prop, kcon, inv, once,
-    parents, accept, weights, noise, source, select, perm, rows, cols, partial, corner, summed, zsum, wbuf,
+    parents, accept, weights, noise, source, select, perm, rows, cols, partial, corner, both, summed, zsum, wbuf,
     send_sem, recv_gather, recv_pick, recv_z, recv_rows, recv_pair, recv_sem, local_sem,
 ):
     group, tile = lax.axis_index("grp"), lax.axis_index("tile")
@@ -299,14 +299,16 @@
             )
             for c in range(2):
                 for j in range(4):
-                    partial[h, j % 2, c, 2 * half + j // 2] = product[64 * c + 16 * j : 64 * c + 16 * j + 16]
-        for i, (across_z, other) in enumerate(((False, True), (True, False), (True, True))):
-            src = partial.at[h, 1 - parity if across_z else parity, 1 - core if other else core]
-            target = device(x, y, beside if across_z else z, 1 - core if other else core)
-            copy(src, corner.at[h, i], send_sem.at[12], recv_pair.at[0, h], target)
+                    partial[h, c, j % 2, 2 * half + j // 2] = product[64 * c + 16 * j : 64 * c + 16 * j + 16]
+        swapped = corner.at[h, pl.ds(0, 2)]
+        copy(partial.at[h, 1 - core], swapped, send_sem.at[12], recv_pair.at[0, h], device(x, y, z, 1 - core))
     for h in range(2):
-        arrived(corner.at[h], recv_pair.at[0, h])
-        summed[h] = (partial[h, parity, core] + corner[h, 0]) + (corner[h, 1] + corner[h, 2])
+        arrived(corner.at[h, pl.ds(0, 2)], recv_pair.at[0, h])
+        both[h] = partial[h, core] + corner[h, 0:2]
+        copy(both.at[h, 1 - parity], corner.at[h, 2], send_sem.at[12], recv_pair.at[2, h], device(x, y, beside, core))
+    for h in range(2):
+        arrived(corner.at[h, 2], recv_pair.at[2, h])
+        summed[h] = both[h, parity] + corner[h, 2]
         for d in (8, 6, 10, 4, 12, 2, 14):
             target = device(x, y, (z + d) % 16, core)
             copy(summed.at[h, ((z + d) % 8) // 2], zsum.at[h, d // 2], send_sem.at[13], recv_pair.at[1, h], target)
@@ -385,10 +387,11 @@
             pltpu.VMEM((4, 4, 2, 32, 128), F32),
             pltpu.VMEM((2, 2, 2, 4, 16, 128), F32),
             pltpu.VMEM((2, 3, 4, 16, 128), F32),
+            pltpu.VMEM((2, 2, 4, 16, 128), F32),
             pltpu.VMEM((2, 4, 16, 128), F32),
             pltpu.VMEM((2, 16, 16, 128), F32),
             pltpu.VMEM((3, 4, 8, 128), F32),
-            dma((15,)), dma((3, CHUNKS)), dma((3, CHUNKS)), dma((2, CHUNKS)), dma((2, 4)), dma((2, 2)), dma((8,)), dma((6,)),
+            dma((15,)), dma((3, CHUNKS)), dma((3, CHUNKS)), dma((2, CHUNKS)), dma((2, 4)), dma((3, 2)), dma((8,)), dma((6,)),
         ],
         compiler_params=pltpu.CompilerParams(collective_id=0, has_side_effects=True),
         name="resample_move",

time: 83.3 us -> 82.4 us (0.989)
  Pallas kernels: 81.9 us -> 81 us
    pallas_call x1, Pallas kernels: 81.1 us -> 80.2 us  [local(): pl.pallas_call(kernel, out_shape=(pltpu.VMEM(block, F32), pltpu.VMEM(bloc...]
where the time goes in v6:
time: 82.4 us; the launch traced here: 82.3 us
  Pallas kernels  81 us (98%)
  between operations  1.29 us (2%)
    pallas_call x1, Pallas kernels, local(): pl.pallas_call(kernel, out_shape=(pltpu.VMEM(block, F32), pltpu.VMEM(bloc...  80.2 us

profile of v6, /device:TPU:1, one launch (start us, length us, event | category | flops | bytes accessed | tf_op | source)
XLA Modules:
  0.0 82.3 jit_solution(8566119481160066638)
XLA Ops:
  1.3 80.2 %resample_move.1 = (f32[8,32,128]{2,1,0:T(8,128)S(1)}, f32[8,32,128]{2,1,0:T(8,128)S(1)}, f32[64,1024]{1,0:T(8,128)S(1)}) custom-call(f32[8,32,128]{2,1,0:T(8,128)} %bitcast.7, f32[8,32,128]{2,1,0:T(8,128)} %bitcast.8, f32[2,8,32,128]{3,2,1,0:T(8,128)} %bitcast.6, f32[8,32,128]{2,1,0:T(8,128)} %source_in.1, s32[32]{0:T(128)} %parents_in.1, s32[2]{0:T(128)} %bitcast.9, ...), custom_call_target="tpu_custom_call" | custom-call | tf_op jit(solution)/shard_map/resample_move/pallas_call | solution.py:357
  81.5 0.8 leave.1
